TPU v7x, 256 devices: a whole 4x4x8 slice. The times are simulated.
256 devices in a mesh: tm: 8 (over x_lo, y), space: 32 (over z, x_hi, core).
Axes of the slice: x: 4 (x_hi: 2, x_lo: 2; x = x_hi * 2 + x_lo), y: 4, z: 8, core: 2. Of those that a mesh axis runs over, the one named last changes fastest.
Arguments:
- guess: float32 [16, 1024, 4096], P('tm', 'space'), may hold values from -6 to 6
- sources: bfloat16 [64, 1024, 4096], P('tm', 'space'), may hold values from -6 to 6
- velocity: bfloat16 [4, 2, 1024, 4096], P(None, None, 'space'), may hold values from -1 to 1
- snapshot: int32 [64], replicated, may hold values from 0 to 3
Outputs:
- c_values: float32 [16, 1024, 4096], P('tm', 'space')
- control_grad: float32 [1024, 4096], P('space', 'tm')
Inputs may be any that keep to these rules, and one draw needn't show every extreme that they name: Each entry names a stored snapshot.
All inputs are finite; a program needn't handle non-finite values.
Results may differ from a plain program's by a relative error of at most 0.0003.
Values may be sent and summed in bfloat16 or wider, within the bound.
No kernel may reach another device: no remote copies, remote signals or barrier semaphores. Data moves between devices by JAX's collectives and lax.ppermute only.
A program may use at most 128 MiB of HBM per device.

v0:
```python
import jax
import jax.numpy as jnp
import numpy as np
from jax import lax
from jax.sharding import PartitionSpec as P

FINE_DIFF = 0.2
FINE_ADV = 0.3
COARSE_DIFF = 0.24
COARSE_ADV = 0.4


def with_halo(array, sides, width):
    for axis, dim in sides:
        count, length = (lax.axis_size(axis), array.shape[dim])
        up = [(i, (i + 1) % count) for i in range(count - 1)]
        down = [(j, i) for i, j in up]
        last = lax.slice_in_dim(array, length - width, length, axis=dim)
        leading = lax.slice_in_dim(array, 0, width, axis=dim)
        before = lax.ppermute(last, axis, up)
        after = lax.ppermute(leading, axis, down)
        array = jnp.concatenate([before, array, after], axis=dim)
    return array


def passed_along(array, axis, by):
    count = lax.axis_size(axis)
    pairs = [(i, i + by) for i in range(count) if 0 <= i + by < count]
    return lax.ppermute(array, axis, pairs)


def shift_east(field):
    return jnp.concatenate([field[..., 1:], jnp.zeros_like(field[..., :1])], -1)


def shift_west(field):
    return jnp.concatenate([jnp.zeros_like(field[..., :1]), field[..., :-1]], -1)


def adjoint_step(state, speeds, diff, adv):
    speed_x = speeds[..., 0, :, :].astype(jnp.float32)
    speed_y = speeds[..., 1, :, :].astype(jnp.float32)
    centre = state[..., 1:-1, :]
    flux_x = speed_x * state
    flux_y = (speed_y * state)[..., 1:-1, :]
    laplace = (
        state[..., 2:, :]
        + state[..., :-2, :]
        + shift_east(centre)
        + shift_west(centre)
        - 4.0 * centre
    )
    advected = flux_x[..., 2:, :] - flux_x[..., :-2, :] + shift_east(flux_y) - shift_west(flux_y)
    return centre + diff * laplace + 0.5 * adv * advected


def body(guess, sources, velocity, snapshot):
    c_points, strip_rows, columns = guess.shape
    steps_dev = sources.shape[0]
    factor = steps_dev // c_points
    snap_count = velocity.shape[0]
    time_blocks = lax.axis_size("tm")
    span_no = lax.axis_index("tm")
    total_steps = steps_dev * time_blocks
    local_snap = lax.dynamic_slice_in_dim(snapshot, span_no * steps_dev, steps_dev)
    flat_speeds = velocity.reshape(snap_count * 2, strip_rows, columns)
    halo_width = 1
    speed_ext = with_halo(flat_speeds, (("space", 1),), 1)
    source_width = 0
    speed_ext = speed_ext.reshape(snap_count, 2, strip_rows + 2 * halo_width, columns)

    def rows_of(field, have, want):
        return field[..., have - want : have - want + strip_rows + 2 * want, :]

    def above(coarse_vals):
        upper = passed_along(coarse_vals[0], "tm", -1)
        return jnp.concatenate([coarse_vals[1:], upper[None]], 0)

    def relax(coarse_vals, with_residual):
        tops = above(coarse_vals)
        state = tops
        reach = 0
        time_total = jnp.zeros((strip_rows, columns), jnp.float32)
        residual = None
        last_offset = 0 if with_residual else 1
        for offset in range(factor - 1, last_offset - 1, -1):
            state = with_halo(state, (("space", 1),), 1)
            reach = 1
            positions = np.arange(c_points) * factor + offset
            picks = local_snap[positions]
            speeds = jnp.take(speed_ext, picks, axis=0)
            updated = adjoint_step(state, rows_of(speeds, halo_width, reach), FINE_DIFF, FINE_ADV)
            reach = reach - 1
            updated = updated + rows_of(sources[positions], source_width, reach).astype(jnp.float32)
            if offset == 0:
                residual = updated - coarse_vals
            else:
                time_total = time_total + jnp.sum(updated[:, reach : reach + strip_rows], 0)
            state = updated
        return (time_total, residual)

    _, residual = relax(guess, True)
    speed_one = rows_of(speed_ext, halo_width, 1)

    def coarse_step(correction, snap_pick):
        extended = with_halo(correction, (("space", 0),), 1)
        speeds = lax.dynamic_index_in_dim(speed_one, snap_pick, 0, keepdims=False)
        return adjoint_step(extended, speeds, COARSE_DIFF, COARSE_ADV)

    zero_field = jnp.zeros((strip_rows, columns), jnp.float32)
    coarse_snaps = local_snap[np.arange(c_points) * factor]

    def local_chain(correction):
        values = []
        for interval in range(c_points - 1, -1, -1):
            correction = coarse_step(correction, coarse_snaps[interval]) + residual[interval]
            values.append(correction)
        return (correction, jnp.stack(values[::-1], 0))

    def round_fn(round_no, incoming):
        lowest, _ = local_chain(incoming)
        return passed_along(lowest, "tm", -1)

    incoming = lax.fori_loop(0, time_blocks - 1, round_fn, zero_field)
    _, corr = local_chain(incoming)
    c_values = guess + corr
    f_total, _ = relax(c_values, False)
    local_total = jnp.sum(c_values, 0) + f_total
    control_grad = (
        lax.psum_scatter(local_total, "tm", scatter_dimension=1, tiled=True) / total_steps
    )
    return (c_values, control_grad)


def solution(mesh):
    in_specs = (P("tm", "space", None), P("tm", "space", None), P(None, None, "space", None), P())
    out_specs = (P("tm", "space", None), P("space", "tm"))
    return jax.shard_map(body, mesh=mesh, in_specs=in_specs, out_specs=out_specs, check_vma=False)
```

profile of v0, /device:TPU:32, one launch (start us, length us, event | category | flops | bytes accessed | tf_op | source)
XLA Modules:
  0.0 516.5 jit_solution(18323332807990863848)
XLA Ops:
  11.1 6.0 %collective-permute-start.6 = (bf16[8,1,4096]{2,0,1:T(8,128)(2,1)S(1)}, bf16[8,1,4096]{2,0,1:T(8,128)(2,1)S(1)}, u32[]{:S(2)}, u32[]{:S(2)}) collective-permute-start(bf16[8,1,4096]{2,0,1:T(8,128)(2,1)S(1)} %copy.103), channel_id=1, source_target_pairs={{1,0},{2,1},{3,2},{4,3},{5,4},{6,5},{7,6},{8,7},{9,8},{10,9},{11,1... | collective-permute-start | bytes 196616 | tf_op jit(solution)/shard_map/ppermute | solution.py:21
  37.3 5.0 pad_maximum_fusion.6
  102.1 4.9 collective-permute-done.13
  114.1 4.9 collective-permute-done.15
  121.7 250.2 %while.12 = (s32[]{:T(128)}, f32[32,4096]{1,0:T(8,128)S(1)}, bf16[1,2,34,4096]{3,2,1,0:T(8,128)(2,1)S(1)}, f32[2,32,4096]{2,1,0:T(8,128)S(1)}, bf16[1,2,34,4096]{3,2,1,0:T(8,128)(2,1)S(1)}, /*index=5*/s32[]{:T(128)}) while((s32[]{:T(128)}, f32[32,4096]{1,0:T(8,128)S(1)}, bf16[1,2,34,4096]{3,2,1,0:T(8,128)(2,1)S(1)}, ...), condition=%wide.region_1.3_spmd, body=%wide.region_0.0_spmd.sunk | while | flops 5603330 | bytes 24835340 | solution.py:124
  126.3 4.8 collective-permute-done.1
  143.7 11.4 %collective-permute-done.4 = f32[32,4096]{1,0:T(8,128)S(1)} collective-permute-done((f32[32,4096]{1,0:T(8,128)S(1)}, f32[32,4096]{1,0:T(8,128)S(1)}, u32[]{:S(2)}, u32[]{:S(2)}) %collective-permute-start.4) | collective-permute-done | bytes 524320 | tf_op jit(solution)/shard_map/while/body/eval_jaxpr/ppermute | solution.py:29
  159.7 5.1 collective-permute-done.1
  177.3 12.8 %collective-permute-done.4 = f32[32,4096]{1,0:T(8,128)S(1)} collective-permute-done((f32[32,4096]{1,0:T(8,128)S(1)}, f32[32,4096]{1,0:T(8,128)S(1)}, u32[]{:S(2)}, u32[]{:S(2)}) %collective-permute-start.4) | collective-permute-done | bytes 524320 | tf_op jit(solution)/shard_map/while/body/eval_jaxpr/ppermute | solution.py:29
  194.7 4.8 collective-permute-done.1
  212.0 13.7 %collective-permute-done.4 = f32[32,4096]{1,0:T(8,128)S(1)} collective-permute-done((f32[32,4096]{1,0:T(8,128)S(1)}, f32[32,4096]{1,0:T(8,128)S(1)}, u32[]{:S(2)}, u32[]{:S(2)}) %collective-permute-start.4) | collective-permute-done | bytes 524320 | tf_op jit(solution)/shard_map/while/body/eval_jaxpr/ppermute | solution.py:29
  230.3 4.8 collective-permute-done.1
  247.7 13.4 %collective-permute-done.4 = f32[32,4096]{1,0:T(8,128)S(1)} collective-permute-done((f32[32,4096]{1,0:T(8,128)S(1)}, f32[32,4096]{1,0:T(8,128)S(1)}, u32[]{:S(2)}, u32[]{:S(2)}) %collective-permute-start.4) | collective-permute-done | bytes 524320 | tf_op jit(solution)/shard_map/while/body/eval_jaxpr/ppermute | solution.py:29
  265.6 4.8 collective-permute-done.1
  282.9 15.0 %collective-permute-done.4 = f32[32,4096]{1,0:T(8,128)S(1)} collective-permute-done((f32[32,4096]{1,0:T(8,128)S(1)}, f32[32,4096]{1,0:T(8,128)S(1)}, u32[]{:S(2)}, u32[]{:S(2)}) %collective-permute-start.4) | collective-permute-done | bytes 524320 | tf_op jit(solution)/shard_map/while/body/eval_jaxpr/ppermute | solution.py:29
  302.5 4.8 collective-permute-done.1
  319.9 15.0 %collective-permute-done.4 = f32[32,4096]{1,0:T(8,128)S(1)} collective-permute-done((f32[32,4096]{1,0:T(8,128)S(1)}, f32[32,4096]{1,0:T(8,128)S(1)}, u32[]{:S(2)}, u32[]{:S(2)}) %collective-permute-start.4) | collective-permute-done | bytes 524320 | tf_op jit(solution)/shard_map/while/body/eval_jaxpr/ppermute | solution.py:29
  339.5 4.8 collective-permute-done.1
  356.8 15.1 %collective-permute-done.4 = f32[32,4096]{1,0:T(8,128)S(1)} collective-permute-done((f32[32,4096]{1,0:T(8,128)S(1)}, f32[32,4096]{1,0:T(8,128)S(1)}, u32[]{:S(2)}, u32[]{:S(2)}) %collective-permute-start.4) | collective-permute-done | bytes 524320 | tf_op jit(solution)/shard_map/while/body/eval_jaxpr/ppermute | solution.py:29
  395.4 14.8 %collective-permute-done.20 = f32[32,4096]{1,0:T(8,128)S(1)} collective-permute-done((f32[32,4096]{1,0:T(8,128)S(1)}, f32[32,4096]{1,0:T(8,128)S(1)}, u32[]{:S(2)}, u32[]{:S(2)}) %collective-permute-start.20) | collective-permute-done | bytes 524320 | tf_op jit(solution)/shard_map/ppermute | solution.py:29
  415.2 4.9 collective-permute-done.22
  428.3 4.9 collective-permute-done.24
  440.5 4.9 collective-permute-done.26
  448.7 59.2 %reduce-scatter.2.cloned.1.call-done = f32[32,512]{1,0:T(8,128)} async-done(((f32[32,4096]{1,0:T(8,128)}), f32[32,512]{1,0:T(8,128)}) %reduce-scatter.2.cloned.1.call-update) | async-done | bytes 65552 | tf_op jit(solution)/shard_map/reduce_scatter | solution.py:130
  (316 shorter events, 256.8 us)
Async XLA Ops:
  7.2 500.7 %reduce-scatter.2.cloned.1.call-start = ((), (), s32[]{:S(2)}) async-start(), calls=%async_computation.1 | async-start | bytes 589824 | tf_op jit(solution)/shard_map/reduce_scatter | solution.py:130
  8.9 28.2 %collective-permute-start.5 = (bf16[8,1,4096]{2,0,1:T(8,128)(2,1)S(1)}, bf16[8,1,4096]{2,0,1:T(8,128)(2,1)S(1)}, u32[]{:S(2)}, u32[]{:S(2)}) collective-permute-start(bf16[8,1,4096]{2,0,1:T(8,128)(2,1)S(1)} %copy.102), channel_id=1, source_target_pairs={{0,1},{1,2},{2,3},{3,4},{4,5},{5,6},{6,7},{7,8},{8,9},{9,10},{10,1... | collective-permute-start | bytes 196616 | tf_op jit(solution)/shard_map/ppermute | solution.py:20
  11.1 26.1 %collective-permute-start.6 = (bf16[8,1,4096]{2,0,1:T(8,128)(2,1)S(1)}, bf16[8,1,4096]{2,0,1:T(8,128)(2,1)S(1)}, u32[]{:S(2)}, u32[]{:S(2)}) collective-permute-start(bf16[8,1,4096]{2,0,1:T(8,128)(2,1)S(1)} %copy.103), channel_id=1, source_target_pairs={{1,0},{2,1},{3,2},{4,3},{5,4},{6,5},{7,6},{8,7},{9,8},{10,9},{11,1... | collective-permute-start | bytes 196616 | tf_op jit(solution)/shard_map/ppermute | solution.py:21
  19.5 49.0 %collective-permute-start.7 = (f32[32,4096]{1,0:T(8,128)}, f32[32,4096]{1,0:T(8,128)}, u32[]{:S(2)}, u32[]{:S(2)}) collective-permute-start(f32[32,4096]{1,0:T(8,128)} %get-tuple-element.186), channel_id=1, source_target_pairs={{32,0},{64,32},{96,64},{128,96},{160,128},{192,160},{224,192},{33,... | collective-permute-start | bytes 1572872 | tf_op jit(solution)/shard_map/ppermute | solution.py:29
  71.5 7.8 %collective-permute-start.9 = (f32[2,1,4096]{2,1,0:T(1,128)S(1)}, f32[2,1,4096]{2,1,0:T(1,128)S(1)}, u32[]{:S(2)}, u32[]{:S(2)}) collective-permute-start(f32[2,1,4096]{2,1,0:T(1,128)S(1)} %get-tuple-element.184), channel_id=1, source_target_pairs={{0,1},{1,2},{2,3},{3,4},{4,5},{5,6},{6,7},{7,8},{8,9},{9,10},{10,1... | collective-permute-start | bytes 98312 | tf_op jit(solution)/shard_map/ppermute | solution.py:20
  87.3 7.6 %collective-permute-start.11 = (f32[2,1,4096]{2,1,0:T(1,128)S(1)}, f32[2,1,4096]{2,1,0:T(1,128)S(1)}, u32[]{:S(2)}, u32[]{:S(2)}) collective-permute-start(f32[2,1,4096]{2,1,0:T(1,128)S(1)} %get-tuple-element.180), channel_id=1, source_target_pairs={{0,1},{1,2},{2,3},{3,4},{4,5},{5,6},{6,7},{7,8},{8,9},{9,10},{10,1... | collective-permute-start | bytes 98312 | tf_op jit(solution)/shard_map/ppermute | solution.py:20
  99.3 7.6 %collective-permute-start.13 = (f32[2,1,4096]{2,1,0:T(1,128)S(1)}, f32[2,1,4096]{2,1,0:T(1,128)S(1)}, u32[]{:S(2)}, u32[]{:S(2)}) collective-permute-start(f32[2,1,4096]{2,1,0:T(1,128)S(1)} %get-tuple-element.176), channel_id=1, source_target_pairs={{0,1},{1,2},{2,3},{3,4},{4,5},{5,6},{6,7},{7,8},{8,9},{9,10},{10,1... | collective-permute-start | bytes 98312 | tf_op jit(solution)/shard_map/ppermute | solution.py:20
  111.3 7.6 %collective-permute-start.15 = (f32[2,1,4096]{2,1,0:T(1,128)S(1)}, f32[2,1,4096]{2,1,0:T(1,128)S(1)}, u32[]{:S(2)}, u32[]{:S(2)}) collective-permute-start(f32[2,1,4096]{2,1,0:T(1,128)S(1)} %get-tuple-element.172), channel_id=1, source_target_pairs={{0,1},{1,2},{2,3},{3,4},{4,5},{5,6},{6,7},{7,8},{8,9},{9,10},{10,1... | collective-permute-start | bytes 98312 | tf_op jit(solution)/shard_map/ppermute | solution.py:20
  142.4 12.7 %collective-permute-start.4 = (f32[32,4096]{1,0:T(8,128)S(1)}, f32[32,4096]{1,0:T(8,128)S(1)}, u32[]{:S(2)}, u32[]{:S(2)}) collective-permute-start(f32[32,4096]{1,0:T(8,128)S(1)} %fusion.177), channel_id=1, source_target_pairs={{32,0},{64,32},{96,64},{128,96},{160,128},{192,160},{224,192},{33,... | collective-permute-start | bytes 1572872 | tf_op jit(solution)/shard_map/while/body/eval_jaxpr/ppermute | solution.py:29
  157.4 7.5 %collective-permute-start.1 = (f32[1,4096]{1,0:T(1,128)S(1)}, f32[1,4096]{1,0:T(1,128)S(1)}, u32[]{:S(2)}, u32[]{:S(2)}) collective-permute-start(f32[1,4096]{1,0:T(1,128)S(1)} %get-tuple-element.256), channel_id=1, source_target_pairs={{0,1},{1,2},{2,3},{3,4},{4,5},{5,6},{6,7},{7,8},{8,9},{9,10},{10,1... | collective-permute-start | bytes 49160 | tf_op jit(solution)/shard_map/while/body/eval_jaxpr/ppermute | solution.py:20
  167.7 7.5 %collective-permute-start.3 = (f32[1,4096]{1,0:T(1,128)S(1)}, f32[1,4096]{1,0:T(1,128)S(1)}, u32[]{:S(2)}, u32[]{:S(2)}) collective-permute-start(f32[1,4096]{1,0:T(1,128)S(1)} %get-tuple-element.264), channel_id=1, source_target_pairs={{0,1},{1,2},{2,3},{3,4},{4,5},{5,6},{6,7},{7,8},{8,9},{9,10},{10,1... | collective-permute-start | bytes 49160 | tf_op jit(solution)/shard_map/while/body/eval_jaxpr/ppermute | solution.py:20
  176.0 14.1 %collective-permute-start.4 = (f32[32,4096]{1,0:T(8,128)S(1)}, f32[32,4096]{1,0:T(8,128)S(1)}, u32[]{:S(2)}, u32[]{:S(2)}) collective-permute-start(f32[32,4096]{1,0:T(8,128)S(1)} %fusion.177), channel_id=1, source_target_pairs={{32,0},{64,32},{96,64},{128,96},{160,128},{192,160},{224,192},{33,... | collective-permute-start | bytes 1572872 | tf_op jit(solution)/shard_map/while/body/eval_jaxpr/ppermute | solution.py:29
  202.4 7.5 %collective-permute-start.3 = (f32[1,4096]{1,0:T(1,128)S(1)}, f32[1,4096]{1,0:T(1,128)S(1)}, u32[]{:S(2)}, u32[]{:S(2)}) collective-permute-start(f32[1,4096]{1,0:T(1,128)S(1)} %get-tuple-element.264), channel_id=1, source_target_pairs={{0,1},{1,2},{2,3},{3,4},{4,5},{5,6},{6,7},{7,8},{8,9},{9,10},{10,1... | collective-permute-start | bytes 49160 | tf_op jit(solution)/shard_map/while/body/eval_jaxpr/ppermute | solution.py:20
  210.7 15.0 %collective-permute-start.4 = (f32[32,4096]{1,0:T(8,128)S(1)}, f32[32,4096]{1,0:T(8,128)S(1)}, u32[]{:S(2)}, u32[]{:S(2)}) collective-permute-start(f32[32,4096]{1,0:T(8,128)S(1)} %fusion.177), channel_id=1, source_target_pairs={{32,0},{64,32},{96,64},{128,96},{160,128},{192,160},{224,192},{33,... | collective-permute-start | bytes 1572872 | tf_op jit(solution)/shard_map/while/body/eval_jaxpr/ppermute | solution.py:29
  238.0 7.5 %collective-permute-start.3 = (f32[1,4096]{1,0:T(1,128)S(1)}, f32[1,4096]{1,0:T(1,128)S(1)}, u32[]{:S(2)}, u32[]{:S(2)}) collective-permute-start(f32[1,4096]{1,0:T(1,128)S(1)} %get-tuple-element.264), channel_id=1, source_target_pairs={{0,1},{1,2},{2,3},{3,4},{4,5},{5,6},{6,7},{7,8},{8,9},{9,10},{10,1... | collective-permute-start | bytes 49160 | tf_op jit(solution)/shard_map/while/body/eval_jaxpr/ppermute | solution.py:20
  246.4 14.7 %collective-permute-start.4 = (f32[32,4096]{1,0:T(8,128)S(1)}, f32[32,4096]{1,0:T(8,128)S(1)}, u32[]{:S(2)}, u32[]{:S(2)}) collective-permute-start(f32[32,4096]{1,0:T(8,128)S(1)} %fusion.177), channel_id=1, source_target_pairs={{32,0},{64,32},{96,64},{128,96},{160,128},{192,160},{224,192},{33,... | collective-permute-start | bytes 1572872 | tf_op jit(solution)/shard_map/while/body/eval_jaxpr/ppermute | solution.py:29
  263.0 7.5 %collective-permute-start.1 = (f32[1,4096]{1,0:T(1,128)S(1)}, f32[1,4096]{1,0:T(1,128)S(1)}, u32[]{:S(2)}, u32[]{:S(2)}) collective-permute-start(f32[1,4096]{1,0:T(1,128)S(1)} %get-tuple-element.256), channel_id=1, source_target_pairs={{0,1},{1,2},{2,3},{3,4},{4,5},{5,6},{6,7},{7,8},{8,9},{9,10},{10,1... | collective-permute-start | bytes 49160 | tf_op jit(solution)/shard_map/while/body/eval_jaxpr/ppermute | solution.py:20
  281.6 16.3 %collective-permute-start.4 = (f32[32,4096]{1,0:T(8,128)S(1)}, f32[32,4096]{1,0:T(8,128)S(1)}, u32[]{:S(2)}, u32[]{:S(2)}) collective-permute-start(f32[32,4096]{1,0:T(8,128)S(1)} %fusion.177), channel_id=1, source_target_pairs={{32,0},{64,32},{96,64},{128,96},{160,128},{192,160},{224,192},{33,... | collective-permute-start | bytes 1572872 | tf_op jit(solution)/shard_map/while/body/eval_jaxpr/ppermute | solution.py:29
  318.6 16.4 %collective-permute-start.4 = (f32[32,4096]{1,0:T(8,128)S(1)}, f32[32,4096]{1,0:T(8,128)S(1)}, u32[]{:S(2)}, u32[]{:S(2)}) collective-permute-start(f32[32,4096]{1,0:T(8,128)S(1)} %fusion.177), channel_id=1, source_target_pairs={{32,0},{64,32},{96,64},{128,96},{160,128},{192,160},{224,192},{33,... | collective-permute-start | bytes 1572872 | tf_op jit(solution)/shard_map/while/body/eval_jaxpr/ppermute | solution.py:29
  355.5 16.4 %collective-permute-start.4 = (f32[32,4096]{1,0:T(8,128)S(1)}, f32[32,4096]{1,0:T(8,128)S(1)}, u32[]{:S(2)}, u32[]{:S(2)}) collective-permute-start(f32[32,4096]{1,0:T(8,128)S(1)} %fusion.177), channel_id=1, source_target_pairs={{32,0},{64,32},{96,64},{128,96},{160,128},{192,160},{224,192},{33,... | collective-permute-start | bytes 1572872 | tf_op jit(solution)/shard_map/while/body/eval_jaxpr/ppermute | solution.py:29
  393.9 16.4 %collective-permute-start.20 = (f32[32,4096]{1,0:T(8,128)S(1)}, f32[32,4096]{1,0:T(8,128)S(1)}, u32[]{:S(2)}, u32[]{:S(2)}) collective-permute-start(f32[32,4096]{1,0:T(8,128)S(1)} %get-tuple-element.168), channel_id=1, source_target_pairs={{32,0},{64,32},{96,64},{128,96},{160,128},{192,160},{224,192},{33,... | collective-permute-start | bytes 1572872 | tf_op jit(solution)/shard_map/ppermute | solution.py:29
  412.2 7.8 %collective-permute-start.22 = (f32[2,1,4096]{2,1,0:T(1,128)S(1)}, f32[2,1,4096]{2,1,0:T(1,128)S(1)}, u32[]{:S(2)}, u32[]{:S(2)}) collective-permute-start(f32[2,1,4096]{2,1,0:T(1,128)S(1)} %get-tuple-element.166), channel_id=1, source_target_pairs={{0,1},{1,2},{2,3},{3,4},{4,5},{5,6},{6,7},{7,8},{8,9},{9,10},{10,1... | collective-permute-start | bytes 98312 | tf_op jit(solution)/shard_map/ppermute | solution.py:20
  425.4 7.8 %collective-permute-start.24 = (f32[2,1,4096]{2,1,0:T(1,128)S(1)}, f32[2,1,4096]{2,1,0:T(1,128)S(1)}, u32[]{:S(2)}, u32[]{:S(2)}) collective-permute-start(f32[2,1,4096]{2,1,0:T(1,128)S(1)} %get-tuple-element.162), channel_id=1, source_target_pairs={{0,1},{1,2},{2,3},{3,4},{4,5},{5,6},{6,7},{7,8},{8,9},{9,10},{10,1... | collective-permute-start | bytes 98312 | tf_op jit(solution)/shard_map/ppermute | solution.py:20
  437.6 7.8 %collective-permute-start.26 = (f32[2,1,4096]{2,1,0:T(1,128)S(1)}, f32[2,1,4096]{2,1,0:T(1,128)S(1)}, u32[]{:S(2)}, u32[]{:S(2)}) collective-permute-start(f32[2,1,4096]{2,1,0:T(1,128)S(1)} %get-tuple-element.158), channel_id=1, source_target_pairs={{0,1},{1,2},{2,3},{3,4},{4,5},{5,6},{6,7},{7,8},{8,9},{9,10},{10,1... | collective-permute-start | bytes 98312 | tf_op jit(solution)/shard_map/ppermute | solution.py:20
  (62 other events, 458.5 us)
Sparse Core Ops, SparseCore 0:
  448.8 59.0 reduce-scatter.1
where the time goes:
time: 522 us; the launch traced here: 516 us
  waiting for transfers between devices  281 us (54%)
  starting transfers between devices  120 us (23%)
  local copies, waits for them, and re-layouts  49 us (9%)
  other arithmetic  46.5 us (9%)
  between operations  19 us (4%)
    ppermute x9, waiting for transfers between devices, passed_along(): return lax.ppermute(array, axis, pairs)  111 us
    ppermute x24, waiting for transfers between devices, with_halo(): before = lax.ppermute(last, axis, up)  110 us
    reduce_scatter x1, waiting for transfers between devices, body(): lax.psum_scatter(local_total, 'tm', scatter_dimension=1, tiled=True)  59.2 us
    ppermute x24, starting transfers between devices, with_halo(): before = lax.ppermute(last, axis, up)  57.8 us
    ppermute x24, starting transfers between devices, with_halo(): after = lax.ppermute(leading, axis, down)  50.7 us
    gather x4, local copies, waits for them, and re-layouts, relax(): speeds = jnp.take(speed_ext, picks, axis=0)  13.6 us
    ppermute x9, starting transfers between devices, passed_along(): return lax.ppermute(array, axis, pairs)  11.8 us
    slice x44, local copies, waits for them, and re-layouts, shift_east(): return jnp.concatenate([field[..., 1:], jnp.zeros_like(field[..., :1])], -1)  10.8 us
  transfers between devices with their start and end apart: 58, of which 32 were waited for; matrix products, arithmetic and copies ran while one was open for 10% of the time, Pallas kernels for 0%

commit v1 on v0

v1 whole, which is shorter than its diff:
```python
import functools

import jax
import jax.numpy as jnp
from jax import lax
from jax.experimental import pallas as pl
from jax.experimental.pallas import tpu as pltpu
from jax.sharding import PartitionSpec as P

FINE_DIFF = 0.2
FINE_ADV = 0.3
COARSE_DIFF = 0.24
COARSE_ADV = 0.4

F32 = jnp.float32
LINK = jnp.float16
LANE = 128
SUB = 8
ROWS = 32
COLS = 4096
CHUNK = 512
WIDE = 640
PAD = COLS + 2 * LANE
NEAR = 40
FAR = 72
NDEV = 8
NCOARSE = 16
TILES = COLS // LANE
LIMIT = 62 * 1024 * 1024

VM = pl.BlockSpec(memory_space=pltpu.VMEM)
SM = pl.BlockSpec(memory_space=pltpu.SMEM)


def halo_tiles():
    return [(j, 1 if j <= 6 else (2 if j < 15 else 3)) for j in range(1, NCOARSE)]


def call(kernel, outs, args, scratch=(), flops=10_000_000):
    specs = [SM if a.dtype == jnp.int32 else VM for a in args]
    nbytes = sum(a.size * a.dtype.itemsize for a in args)
    return pl.pallas_call(
        kernel,
        out_shape=outs,
        in_specs=specs,
        out_specs=jax.tree.map(lambda _: VM, outs),
        scratch_shapes=list(scratch),
        compiler_params=pltpu.CompilerParams(vmem_limit_bytes=LIMIT),
        cost_estimate=pl.CostEstimate(flops=flops, bytes_accessed=nbytes, transcendentals=0),
    )(*args)


def sub_iota(cols):
    return lax.broadcasted_iota(jnp.int32, (SUB, cols), 0)


def lane_iota(rows):
    return lax.broadcasted_iota(jnp.int32, (rows, LANE), 1)


def roll4(x):
    return pltpu.roll(x, 4, 0)


def up(x):
    return pltpu.roll(x, x.shape[0] - 1, 0)


def down(x):
    return pltpu.roll(x, 1, 0)


def east(x):
    return pltpu.roll(x, x.shape[1] - 1, 1)


def west(x):
    return pltpu.roll(x, 1, 1)


def pack_inputs(guess, sources, velocity, out_a, out_b):
    t = lax.axis_index("tm")
    odd = lax.rem(lax.axis_index("space"), 2) == 1
    low = sub_iota(COLS) < 4

    def put(n, top, bottom):
        out_a[n * SUB : (n + 1) * SUB, :] = jnp.where(odd, top, bottom).astype(jnp.bfloat16)
        out_b[n * SUB : (n + 1) * SUB, :] = jnp.where(odd, bottom, top).astype(jnp.bfloat16)

    def pair(n, read_x, read_y):
        x0, y0 = read_x(0), read_y(0)
        x3, y3 = read_x(24), read_y(24)
        put(n, jnp.where(low, x0, roll4(y0)), jnp.where(low, roll4(x3), y3))

    def rows(ref, *at):
        return lambda r: ref[(*at, pl.ds(r, SUB), slice(None))].astype(F32)

    for k in range(4):
        pair(k, rows(velocity, k, 0), rows(velocity, k, 1))
    for i, n in enumerate((3, 2, 1)):
        pair(4 + i, rows(sources, n), rows(sources, n + 4))
    pair(7, rows(guess, 1), rows(guess, 0))

    base = pl.multiple_of(t * CHUNK, LANE)
    left = pl.multiple_of(jnp.maximum(t * CHUNK - LANE, 0), LANE)
    right = pl.multiple_of(jnp.minimum(t * CHUNK + CHUNK, COLS - LANE), LANE)
    half = lane_iota(SUB) < 64
    sub = sub_iota(LANE)

    def wide(k, c, r, l):
        if l < 4:
            return velocity[k, c, pl.ds(r, SUB), pl.ds(base + l * LANE, LANE)].astype(F32)
        a = velocity[k, c, pl.ds(r, SUB), pl.ds(right, LANE)].astype(F32)
        b = velocity[k, c, pl.ds(r, SUB), pl.ds(left, LANE)].astype(F32)
        return jnp.where(half, a, b)

    def place(q, top, bottom):
        r, l = 8 + q // TILES, q % TILES
        at = (slice(r * SUB, (r + 1) * SUB), slice(l * LANE, (l + 1) * LANE))
        out_a[at] = jnp.where(odd, top, bottom).astype(jnp.bfloat16)
        out_b[at] = jnp.where(odd, bottom, top).astype(jnp.bfloat16)

    for k in range(4):
        for c in range(2):
            for l in range(5):
                for half_no in range(2):
                    q = ((k * 2 + c) * 2 + half_no) * 5 + l
                    place(q, wide(k, c, 8 * half_no, l), wide(k, c, 24 - 8 * half_no, l))
    for l in range(5):
        top = jnp.zeros((SUB, LANE), F32)
        bottom = top
        for k in range(4):
            a, b = wide(k, 0, 16, l), wide(k, 0, 8, l)
            top = jnp.where(sub == k, pltpu.roll(a, k, 0) if k else a, top)
            bottom = jnp.where(sub == k, pltpu.roll(b, k + 1, 0), bottom)
        place(80 + l, top, bottom)
    for q in range(85, 3 * TILES):
        place(q, jnp.zeros((SUB, LANE), F32), jnp.zeros((SUB, LANE), F32))


def swap(buf_a, buf_b):
    count = lax.axis_size("space")
    pairs_b = [(i, i + 1) for i in range(1, count - 1, 2)]
    pairs_b = pairs_b + [(j, i) for i, j in pairs_b]
    pairs_a = [(i, i ^ 1) for i in range(count)]
    got_b = lax.ppermute(buf_b, "space", pairs_b)
    got_a = lax.ppermute(buf_a, "space", pairs_a)
    return got_a, got_b


def fine_ext(p, l0, vel, snap, width):
    mid = pl.multiple_of(l0 + LANE, LANE)
    pe = p[:, pl.ds(mid, width + LANE)]
    pw = p[:, pl.ds(pl.multiple_of(l0, LANE), width + LANE)]
    pc = p[:, pl.ds(mid, width)]
    ax = vel[snap, 0, :, pl.ds(mid, width)]
    ye = vel[snap, 1, :, pl.ds(mid, width + LANE)]
    yw = vel[snap, 1, :, pl.ds(pl.multiple_of(l0, LANE), width + LANE)]
    u = FINE_DIFF * pc
    wx = ax * pc
    out = (1.0 - 4.0 * FINE_DIFF) * pc + up(u + wx) + down(u - wx)
    ge = (FINE_DIFF + ye) * pe
    gw = (FINE_DIFF - yw) * pw
    return out + east(ge)[:, :width] + west(gw)[:, LANE:]


def first_relax(snapshot, guess, sources, velocity, got_a, got_b, pay, base, vel, s_halo, pa, pb, acc, res):
    t = lax.axis_index("tm")
    s = lax.axis_index("space")
    odd = lax.rem(s, 2) == 1
    first = t * 8
    low = sub_iota(COLS) < 4
    has_above = (s > 0).astype(F32)
    has_below = (s < lax.axis_size("space") - 1).astype(F32)
    inner = (t > 0).astype(F32)

    def halves(n):
        a = got_a[n * SUB : (n + 1) * SUB, :].astype(F32)
        b = got_b[n * SUB : (n + 1) * SUB, :].astype(F32)
        below, above = jnp.where(odd, b, a), jnp.where(odd, a, b)
        return jnp.where(low, below, roll4(above)), jnp.where(low, roll4(below), above)

    zero = jnp.zeros((NEAR, LANE), F32)
    for buf in (pa, pb):
        buf[:, :LANE] = zero
        buf[:, PAD - LANE :] = zero
    for n in range(4):
        res[n, :, :LANE] = zero[:ROWS]
        res[n, :, PAD - LANE :] = zero[:ROWS]
    mid = slice(LANE, PAD - LANE)
    for k in range(4):
        hx, hy = halves(k)
        for c, h in ((0, hx), (1, hy)):
            vel[k, c, :, :LANE] = zero
            vel[k, c, :, PAD - LANE :] = zero
            vel[k, c, :ROWS, mid] = (0.5 * FINE_ADV) * velocity[k, c].astype(F32)
            vel[k, c, ROWS:, mid] = (0.5 * FINE_ADV) * h
    for i, n in enumerate((3, 2, 1)):
        hx, hy = halves(4 + i)
        s_halo[n] = hx
        s_halo[n + 4] = hy
    g1, g0 = halves(7)

    width = CHUNK
    sub = sub_iota(width)
    edge = jnp.where(sub < 4, has_below, has_above)

    def step(src, dst, snap, source, accumulate):
        def go(i, carry):
            l0 = i * width
            out = fine_ext(src, l0, vel, snap, width)
            at = pl.ds(pl.multiple_of(l0, LANE), width)
            own, far = out[:ROWS], out[ROWS:] * edge
            if source is not None:
                own = own + sources[source, :, at].astype(F32)
                far = far + s_halo[source, :, at]
            to = pl.ds(pl.multiple_of(l0 + LANE, LANE), width)
            dst[:ROWS, to] = own
            dst[ROWS:, to] = far
            acc[:, at] = acc[:, at] + own
            return carry

        lax.fori_loop(0, COLS // width, go, 0)

    def last(src, snap, source, n, level):
        def go(i, carry):
            l0 = i * width
            own = fine_ext(src, l0, vel, snap, width)[:ROWS]
            at = pl.ds(pl.multiple_of(l0, LANE), width)
            to = pl.ds(pl.multiple_of(l0 + LANE, LANE), width)
            if source is not None:
                own = own + sources[source, :, at].astype(F32)
                base[level, :, at] = own
                own = own - guess[level, :, at]
            res[n, :, to] = own
            return carry

        lax.fori_loop(0, COLS // width, go, 0)

    acc[...] = guess[0] + guess[1]
    pa[:ROWS, mid] = guess[1]
    pa[ROWS:, mid] = g1
    step(pa, pb, snapshot[first + 3], 3, True)
    step(pb, pa, snapshot[first + 2], 2, True)
    step(pa, pb, snapshot[first + 1], 1, True)
    last(pb, snapshot[first], 0, 0, 0)
    pa[:ROWS, mid] = sources[7].astype(F32)
    pa[ROWS:, mid] = s_halo[7]
    acc[...] = acc[...] + sources[7].astype(F32)
    step(pa, pb, snapshot[first + 6], 6, True)
    step(pb, pa, snapshot[first + 5], 5, True)
    last(pa, snapshot[first + 4], 4, 1, 1)
    pa[:ROWS, mid] = guess[0] * inner
    pa[ROWS:, mid] = g0 * inner
    before = jnp.maximum(first - 4, 0)
    step(pa, pb, snapshot[before + 3], None, True)
    step(pb, pa, snapshot[before + 2], None, True)
    step(pa, pb, snapshot[before + 1], None, True)
    last(pb, snapshot[before], None, 2, None)
    res[3, :, mid] = acc[...]

    half = lane_iota(ROWS) < 64
    for n in range(4):
        for d in range(NDEV):
            at = LANE + d * CHUNK
            pay[d, n, :, :CHUNK] = res[n, :, at : at + CHUNK]
            right = res[n, :, at + CHUNK : at + CHUNK + LANE]
            left = res[n, :, at - LANE : at]
            pay[d, n, :, CHUNK:] = jnp.where(half, right, left)


def level_rows(got, j, r):
    t, u = divmod(j, 2)
    value = got[t, u, r : r + SUB, :]
    if u == 1 and t + 1 < NDEV:
        value = value + got[t + 1, 2, r : r + SUB, :]
    return value


def pack_residual(got, out_a, out_b):
    odd = lax.rem(lax.axis_index("space"), 2) == 1
    n = 0
    for j, count in halo_tiles():
        for i in range(count):
            top, bottom = level_rows(got, j, 8 * i), level_rows(got, j, 24 - 8 * i)
            out_a[n * SUB : (n + 1) * SUB, :] = jnp.where(odd, top, bottom)
            out_b[n * SUB : (n + 1) * SUB, :] = jnp.where(odd, bottom, top)
            n += 1


def coarse_solve(snapshot, got, velocity, in_a, in_b, got_a, got_b, back, near, vnear, part, vel, res, mask):
    t = lax.axis_index("tm")
    s = lax.axis_index("space")
    odd = lax.rem(s, 2) == 1
    has_above = (s > 0).astype(F32)
    has_below = (s < lax.axis_size("space") - 1).astype(F32)
    has_left = (t > 0).astype(F32)
    has_right = (t < lax.axis_size("tm") - 1).astype(F32)
    row = lax.broadcasted_iota(jnp.int32, (FAR, WIDE), 0)
    col = lax.broadcasted_iota(jnp.int32, (FAR, WIDE), 1)
    in_rows = jnp.where(row < ROWS, 1.0, jnp.where(row < 52, has_below, has_above))
    in_cols = jnp.where(col < CHUNK, 1.0, jnp.where(col < CHUNK + 64, has_right, has_left))
    mask[...] = in_rows * in_cols

    base = pl.multiple_of(t * CHUNK, LANE)
    left = pl.multiple_of(jnp.maximum(t * CHUNK - LANE, 0), LANE)
    right = pl.multiple_of(jnp.minimum(t * CHUNK + CHUNK, COLS - LANE), LANE)
    half = lane_iota(ROWS) < 64
    sub = sub_iota(LANE)
    low = sub < 4

    def tile(q):
        r, l = 8 + q // TILES, q % TILES
        at = (slice(r * SUB, (r + 1) * SUB), slice(l * LANE, (l + 1) * LANE))
        a, b = in_a[at].astype(F32), in_b[at].astype(F32)
        return jnp.where(odd, b, a), jnp.where(odd, a, b)

    fine = 0.5 * FINE_ADV
    coarse = 0.5 * COARSE_ADV
    for k in range(4):
        for c in range(2):
            for l in range(5):
                lanes = slice(l * LANE, (l + 1) * LANE)
                if l < 4:
                    own = velocity[k, c, :, pl.ds(base + l * LANE, LANE)].astype(F32)
                else:
                    own = jnp.where(
                        half,
                        velocity[k, c, :, pl.ds(right, LANE)].astype(F32),
                        velocity[k, c, :, pl.ds(left, LANE)].astype(F32),
                    )
                q = (k * 2 + c) * 10 + l
                below0, above0 = tile(q)
                below1, above1 = tile(q + 5)
                edge = jnp.zeros((SUB, LANE), F32)
                if c == 0:
                    below, above = tile(80 + l)
                    shifted = pltpu.roll(below, SUB - k, 0) if k else below
                    edge = jnp.where(sub == 0, shifted, edge)
                    edge = jnp.where(sub == 7, pltpu.roll(above, 7 - k, 0), edge)
                vel[k, c, :ROWS, lanes] = coarse * own
                vel[k, c, 32:40, lanes] = coarse * below0
                vel[k, c, 40:48, lanes] = coarse * below1
                vel[k, c, 48:56, lanes] = coarse * edge
                vel[k, c, 56:64, lanes] = coarse * above1
                vel[k, c, 64:72, lanes] = coarse * above0
                vnear[k, c, :ROWS, lanes] = fine * own
                vnear[k, c, ROWS:, lanes] = fine * jnp.where(low, below0, above0)

    n = 0
    low_w = sub_iota(WIDE) < 4
    empty = jnp.zeros((SUB, WIDE), F32)
    for j, count in halo_tiles():
        tiles = []
        for i in range(count):
            a, b = got_a[n * SUB : (n + 1) * SUB, :], got_b[n * SUB : (n + 1) * SUB, :]
            tiles.append((jnp.where(odd, b, a), jnp.where(odd, a, b)))
            n += 1
        res[j, 32:40, :] = tiles[0][0]
        res[j, 64:72, :] = tiles[0][1]
        res[j, 40:48, :] = tiles[1][0] if count > 1 else empty
        res[j, 56:64, :] = tiles[1][1] if count > 1 else empty
        res[j, 48:56, :] = jnp.where(low_w, *tiles[2]) if count > 2 else empty
    res[0, ROWS:, :] = jnp.zeros((FAR - ROWS, WIDE), F32)
    for j in range(NCOARSE):
        res[j, :ROWS, :] = got[j // 2, j % 2]

    total = got[0, 3, :, :CHUNK]
    for d in range(1, NDEV):
        total = total + got[d, 3, :, :CHUNK]
    part[...] = total

    def send(j, p, e):
        back[j // 2, j % 2] = e[:ROWS, :CHUNK]
        near[j, :ROWS, :] = p[:ROWS]
        near[j, ROWS:, :] = jnp.where(low_w, p[32:40], p[64:72])
        part[...] = part[...] + p[:ROWS, :CHUNK]

    p = res[NCOARSE - 1]
    send(NCOARSE - 1, p, jnp.zeros_like(p))
    for j in range(NCOARSE - 2, -1, -1):
        snap = snapshot[4 * j]
        ax, ay = vel[snap, 0], vel[snap, 1]
        u = COARSE_DIFF * p
        wx = ax * p
        wy = ay * p
        e = (1.0 - 4.0 * COARSE_DIFF) * p + up(u + wx) + down(u - wx) + east(u + wy) + west(u - wy)
        e = e * mask[...]
        if j % 2 == 1:
            head = e[:ROWS] + got[j // 2 + 1, 2]
            e = jnp.concatenate([head, e[ROWS:]], 0)
        p = e + res[j]
        send(j, p, e)


def second_relax(snapshot, near, vnear, part, grad, acc):
    t = lax.axis_index("tm")
    s = lax.axis_index("space")
    has_above = (s > 0).astype(F32)
    has_below = (s < lax.axis_size("space") - 1).astype(F32)
    has_left = (t > 0).astype(F32)
    has_right = (t < lax.axis_size("tm") - 1).astype(F32)
    row = lax.broadcasted_iota(jnp.int32, (NEAR, WIDE), 0)
    col = lax.broadcasted_iota(jnp.int32, (NEAR, WIDE), 1)
    in_rows = jnp.where(row < ROWS, 1.0, jnp.where(row < 36, has_below, has_above))
    in_cols = jnp.where(col < CHUNK, 1.0, jnp.where(col < CHUNK + 64, has_right, has_left))
    mask = in_rows * in_cols
    acc[...] = part[...]

    def interval(j, carry):
        p = near[j + 1]
        for k in (3, 2, 1):
            snap = snapshot[4 * j + k]
            ax, ay = vnear[snap, 0], vnear[snap, 1]
            u = FINE_DIFF * p
            wx = ax * p
            wy = ay * p
            e = (1.0 - 4.0 * FINE_DIFF) * p + up(u + wx) + down(u - wx) + east(u + wy) + west(u - wy)
            p = e * mask
            acc[...] = acc[...] + p[:ROWS, :CHUNK]
        return carry

    lax.fori_loop(0, NCOARSE - 1, interval, 0)
    grad[...] = acc[...] * (1.0 / 64.0)


def finish(base, got, out):
    for d in range(NDEV):
        at = slice(d * CHUNK, (d + 1) * CHUNK)
        for u in range(2):
            out[u, :, at] = base[u, :, at] + got[d, u]


def body(guess, sources, velocity, snapshot):
    shape = jax.ShapeDtypeStruct
    bf = jnp.bfloat16
    packed = shape((88, COLS), bf)
    send_a, send_b = call(pack_inputs, (packed, packed), (guess, sources, velocity))
    in_a, in_b = swap(send_a, send_b)
    pay, base = call(
        first_relax,
        (shape((NDEV, 4, ROWS, WIDE), F32), shape((2, ROWS, COLS), F32)),
        (snapshot, guess, sources, velocity, in_a, in_b),
        (
            pltpu.VMEM((4, 2, NEAR, PAD), F32),
            pltpu.VMEM((8, SUB, COLS), F32),
            pltpu.VMEM((NEAR, PAD), F32),
            pltpu.VMEM((NEAR, PAD), F32),
            pltpu.VMEM((ROWS, COLS), F32),
            pltpu.VMEM((4, ROWS, PAD), F32),
        ),
    )
    got = lax.all_to_all(pay.astype(LINK), "tm", 0, 0, tiled=False).astype(F32)
    tiles = sum(count for _, count in halo_tiles())
    edges = shape((tiles * SUB, WIDE), F32)
    send_a, send_b = call(pack_residual, (edges, edges), (got,))
    got_a, got_b = swap(send_a.astype(LINK), send_b.astype(LINK))
    back, near, vnear, part = call(
        coarse_solve,
        (
            shape((NDEV, 2, ROWS, CHUNK), F32),
            shape((NCOARSE, NEAR, WIDE), F32),
            shape((4, 2, NEAR, WIDE), F32),
            shape((ROWS, CHUNK), F32),
        ),
        (snapshot, got, velocity, in_a, in_b, got_a.astype(F32), got_b.astype(F32)),
        (
            pltpu.VMEM((4, 2, FAR, WIDE), F32),
            pltpu.VMEM((NCOARSE, FAR, WIDE), F32),
            pltpu.VMEM((FAR, WIDE), F32),
        ),
    )
    returned = lax.all_to_all(back.astype(LINK), "tm", 0, 0, tiled=False)
    grad = call(
        second_relax,
        shape((ROWS, CHUNK), F32),
        (snapshot, near, vnear, part),
        (pltpu.VMEM((ROWS, CHUNK), F32),),
    )
    c_values = call(finish, shape((2, ROWS, COLS), F32), (base, returned.astype(F32)))
    return c_values, grad


def solution(mesh):
    in_specs = (P("tm", "space", None), P("tm", "space", None), P(None, None, "space", None), P())
    out_specs = (P("tm", "space", None), P("space", "tm"))
    return jax.shard_map(body, mesh=mesh, in_specs=in_specs, out_specs=out_specs, check_vma=False)
```

time: 522 us -> 108 us (0.21)
  the two profiles are of different devices: /device:TPU:32 before, /device:TPU:129 now
where the time goes in v1:
time: 108 us
  Pallas kernels  42 us (39%)
  waiting for transfers between devices  22.2 us (21%)
  blocking collectives  18.9 us (17%)
  starting transfers between devices  12.2 us (11%)
  other arithmetic  10.9 us (10%)
    pallas_call x6, Pallas kernels, call(): pl.pallas_call(kernel, out_shape=outs, in_specs=specs, out_specs=jax.tree...  42 us
    ppermute x2, waiting for transfers between devices, swap(): got_b = lax.ppermute(buf_b, 'space', pairs_b)  22 us
    all_to_all x1, blocking collectives, body(): got = lax.all_to_all(pay.astype(LINK), 'tm', 0, 0, tiled=False).astype(F32)  18.9 us
    ppermute x2, starting transfers between devices, swap(): got_b = lax.ppermute(buf_b, 'space', pairs_b)  7.95 us
    convert_element_type x2, other arithmetic, body(): got = lax.all_to_all(pay.astype(LINK), 'tm', 0, 0, tiled=False).astype(F32)  3.78 us
    all_to_all x1, starting transfers between devices, body(): returned = lax.all_to_all(back.astype(LINK), 'tm', 0, 0, tiled=False)  3.49 us
  transfers between devices with their start and end apart: 5, of which 3 were waited for; matrix products, arithmetic and copies ran while one was open for 2% of the time, Pallas kernels for 7%

profile of v1, /device:TPU:129, one launch (start us, length us, event | category | flops | bytes accessed | tf_op | source)
XLA Modules:
  0.0 107.8 jit_solution(5024027341767572066)
XLA Ops:
  0.6 4.1 %shard_map.59 = (bf16[88,4096]{1,0:T(8,128)(2,1)}, bf16[88,4096]{1,0:T(8,128)(2,1)}) custom-call(f32[2,32,4096]{2,1,0:T(8,128)} %guess.3, bf16[8,32,4096]{2,1,0:T(8,128)(2,1)} %sources.3, bf16[4,2,32,4096]{3,2,1,0:T(8,128)(2,1)} %velocity.5), custom_call_target="tpu_custom_call" | custom-call | flops 10000000 | bytes 5242880 | tf_op jit(solution)/shard_map/pallas_call | solution.py:42
  4.7 0.7 collective-permute-start
  5.4 4.5 %collective-permute-start.1 = (bf16[88,4096]{1,0:T(8,128)(2,1)}, bf16[88,4096]{1,0:T(8,128)(2,1)S(1)}, u32[]{:S(2)}, u32[]{:S(2)}) collective-permute-start(bf16[88,4096]{1,0:T(8,128)(2,1)} %get-tuple-element.13), channel_id=1, source_target_pairs={{1,2},{3,4},{5,6},{7,8},{9,10},{11,12},{13,14},{15,16},{17,18},{19... | collective-permute-start | bytes 2162696 | tf_op jit(solution)/shard_map/ppermute | solution.py:146
  10.0 17.5 %collective-permute-done.1.got_b.in_b = bf16[88,4096]{1,0:T(8,128)(2,1)S(1)} collective-permute-done((bf16[88,4096]{1,0:T(8,128)(2,1)}, bf16[88,4096]{1,0:T(8,128)(2,1)S(1)}, u32[]{:S(2)}, u32[]{:S(2)}) %collective-permute-start.1) | collective-permute-done | bytes 720928 | tf_op jit(solution)/shard_map/ppermute | solution.py:146
  27.5 0.9 copy-done.1
  28.3 16.7 %shard_map.60 = (f32[8,4,32,640]{3,2,1,0:T(8,128)}, f32[2,32,4096]{2,1,0:T(8,128)}) custom-call(s32[64]{0:T(128)} %snapshot.5, f32[2,32,4096]{2,1,0:T(8,128)} %guess.3, bf16[8,32,4096]{2,1,0:T(8,128)(2,1)} %sources.3, bf16[4,2,32,4096]{3,2,1,0:T(8,128)(2,1)} %velocity.5, bf16[88,4096]{1,0:T(8,128)(2,1)} %copy-done, bf16[88,4096]{1,0:T(8,128)(2,1)} %copy-done.1), custom_call_target="tpu_custom_call" | custom-call | flops 10000000 | bytes 6684928 | tf_op jit(solution)/shard_map/pallas_call | solution.py:42
  45.0 2.0 %convert_element_type.24 = f16[8,4,32,640]{3,2,1,0:T(8,128)(2,1)S(1)} convert(f32[8,4,32,640]{3,2,1,0:T(8,128)} %get-tuple-element.15) | non-fusion elementwise | flops 655360 | bytes 3932160 | tf_op jit(solution)/shard_map/convert_element_type | solution.py:453
  47.0 18.9 %all_to_all.10 = f16[8,4,32,640]{3,2,1,0:T(8,128)(2,1)S(1)} all-to-all(f16[8,4,32,640]{3,2,1,0:T(8,128)(2,1)S(1)} %convert_element_type.24), channel_id=1, replica_groups=mesh['tm'=8,'space'=32] {'tm'}, dimensions={0} | all-to-all | bytes 2621440 | tf_op jit(solution)/shard_map/all_to_all | solution.py:453
  65.9 1.8 %convert_element_type.25.got = f32[8,4,32,640]{3,2,1,0:T(8,128)} convert(f16[8,4,32,640]{3,2,1,0:T(8,128)(2,1)S(1)} %all_to_all.10) | non-fusion elementwise | flops 655360 | bytes 3932160 | tf_op jit(solution)/shard_map/convert_element_type | solution.py:453
  67.7 2.8 %shard_map.61 = (f32[200,640]{1,0:T(8,128)}, f32[200,640]{1,0:T(8,128)}) custom-call(f32[8,4,32,640]{3,2,1,0:T(8,128)} %convert_element_type.25.got), custom_call_target="tpu_custom_call" | custom-call | flops 10000000 | bytes 2621440 | tf_op jit(solution)/shard_map/pallas_call | solution.py:42
  70.5 1.1 convert_element_type.28
  71.6 3.4 %collective-permute-start.3 = (f16[200,640]{1,0:T(8,128)(2,1)S(1)}, f16[200,640]{1,0:T(8,128)(2,1)S(1)}, u32[]{:S(2)}, u32[]{:S(2)}) collective-permute-start(f16[200,640]{1,0:T(8,128)(2,1)S(1)} %convert_element_type.28), channel_id=1, source_target_pairs={{1,2},{3,4},{5,6},{7,8},{9,10},{11,12},{13,14},{15,16},{17,18},{19... | collective-permute-start | bytes 768008 | tf_op jit(solution)/shard_map/ppermute | solution.py:146
  75.0 1.1 convert_element_type.26
  76.1 0.1 collective-permute-start.2
  76.2 4.5 %collective-permute-done.3 = f16[200,640]{1,0:T(8,128)(2,1)S(1)} collective-permute-done((f16[200,640]{1,0:T(8,128)(2,1)S(1)}, f16[200,640]{1,0:T(8,128)(2,1)S(1)}, u32[]{:S(2)}, u32[]{:S(2)}) %collective-permute-start.3) | collective-permute-done | bytes 256032 | tf_op jit(solution)/shard_map/ppermute | solution.py:146
  80.7 0.9 convert_element_type.29.got_b
  81.6 0.8 convert_element_type.27.got_a
  82.4 7.8 %shard_map.62 = (f32[8,2,32,512]{3,2,1,0:T(8,128)}, f32[16,40,640]{2,1,0:T(8,128)}, f32[4,2,40,640]{3,2,1,0:T(8,128)}, f32[32,512]{1,0:T(8,128)}) custom-call(s32[64]{0:T(128)} %snapshot.5, f32[8,4,32,640]{3,2,1,0:T(8,128)} %convert_element_type.25.got, bf16[4,2,32,4096]{3,2,1,0:T(8,128)(2,1)} %velocity.5, bf16[88,4096]{1,0:T(8,128)(2,1)} %copy-done, ...), custom_call_target="tpu_custom_call" | custom-call | flops 10000000 | bytes 7184640 | tf_op jit(solution)/shard_map/pallas_call | solution.py:42
  90.2 2.1 %convert_element_type.30 = f16[8,2,32,512]{3,2,1,0:T(8,128)(2,1)} convert(f32[8,2,32,512]{3,2,1,0:T(8,128)} %get-tuple-element.18) | non-fusion elementwise | flops 262144 | bytes 1572864 | tf_op jit(solution)/shard_map/convert_element_type | solution.py:473
  92.3 3.5 %all-to-all-start.1 = ((f16[8,2,32,512]{3,2,1,0:T(8,128)(2,1)}), f16[8,2,32,512]{3,2,1,0:T(8,128)(2,1)S(1)}, u32[]{:S(2)}, u32[]{:S(2)}) async-start(f16[8,2,32,512]{3,2,1,0:T(8,128)(2,1)} %convert_element_type.30), calls=%async_computation.1 | async-start | bytes 1048576 | tf_op jit(solution)/shard_map/all_to_all | solution.py:473
  95.8 8.0 %shard_map.64 = f32[32,512]{1,0:T(8,128)} custom-call(s32[64]{0:T(128)} %snapshot.5, f32[16,40,640]{2,1,0:T(8,128)} %get-tuple-element.19.near, f32[4,2,40,640]{3,2,1,0:T(8,128)} %get-tuple-element.20.vnear, f32[32,512]{1,0:T(8,128)} %get-tuple-element.21.part), custom_call_target="tpu_custom_call" | custom-call | flops 10000000 | bytes 2523392 | tf_op jit(solution)/shard_map/pallas_call | solution.py:42
  103.9 0.2 all-to-all-done.1
  104.1 1.1 %convert_element_type.31.got = f32[8,2,32,512]{3,2,1,0:T(8,128)} convert(f16[8,2,32,512]{3,2,1,0:T(8,128)(2,1)S(1)} %all-to-all-done.1) | non-fusion elementwise | flops 262144 | bytes 1572864 | tf_op jit(solution)/shard_map/convert_element_type | solution.py:480
  105.2 2.6 %shard_map.63 = f32[2,32,4096]{2,1,0:T(8,128)} custom-call(f32[2,32,4096]{2,1,0:T(8,128)} %get-tuple-element.14.base, f32[8,2,32,512]{3,2,1,0:T(8,128)} %convert_element_type.31.got), custom_call_target="tpu_custom_call" | custom-call | flops 10000000 | bytes 2097152 | tf_op jit(solution)/shard_map/pallas_call | solution.py:42
  (5 shorter events, 0.0 us)
Async XLA Ops:
  4.7 5.2 %collective-permute-start = (bf16[88,4096]{1,0:T(8,128)(2,1)}, bf16[88,4096]{1,0:T(8,128)(2,1)S(1)}, u32[]{:S(2)}, u32[]{:S(2)}) collective-permute-start(bf16[88,4096]{1,0:T(8,128)(2,1)} %get-tuple-element.12), channel_id=1, source_target_pairs={{0,1},{1,0},{2,3},{3,2},{4,5},{5,4},{6,7},{7,6},{8,9},{9,8},{10,11... | collective-permute-start | bytes 2162696 | tf_op jit(solution)/shard_map/ppermute | solution.py:147
  5.4 22.0 %collective-permute-start.1 = (bf16[88,4096]{1,0:T(8,128)(2,1)}, bf16[88,4096]{1,0:T(8,128)(2,1)S(1)}, u32[]{:S(2)}, u32[]{:S(2)}) collective-permute-start(bf16[88,4096]{1,0:T(8,128)(2,1)} %get-tuple-element.13), channel_id=1, source_target_pairs={{1,2},{3,4},{5,6},{7,8},{9,10},{11,12},{13,14},{15,16},{17,18},{19... | collective-permute-start | bytes 2162696 | tf_op jit(solution)/shard_map/ppermute | solution.py:146
  10.0 17.5 %copy-start = (bf16[88,4096]{1,0:T(8,128)(2,1)}, bf16[88,4096]{1,0:T(8,128)(2,1)S(1)}, u32[]{:S(2)}) copy-start(bf16[88,4096]{1,0:T(8,128)(2,1)S(1)} %collective-permute-done.got_a.in_a) | copy-start | bytes 2162692
  27.5 0.9 copy-start.1
  71.6 9.1 %collective-permute-start.3 = (f16[200,640]{1,0:T(8,128)(2,1)S(1)}, f16[200,640]{1,0:T(8,128)(2,1)S(1)}, u32[]{:S(2)}, u32[]{:S(2)}) collective-permute-start(f16[200,640]{1,0:T(8,128)(2,1)S(1)} %convert_element_type.28), channel_id=1, source_target_pairs={{1,2},{3,4},{5,6},{7,8},{9,10},{11,12},{13,14},{15,16},{17,18},{19... | collective-permute-start | bytes 768008 | tf_op jit(solution)/shard_map/ppermute | solution.py:146
  76.1 5.5 %collective-permute-start.2 = (f16[200,640]{1,0:T(8,128)(2,1)S(1)}, f16[200,640]{1,0:T(8,128)(2,1)S(1)}, u32[]{:S(2)}, u32[]{:S(2)}) collective-permute-start(f16[200,640]{1,0:T(8,128)(2,1)S(1)} %convert_element_type.26), channel_id=1, source_target_pairs={{0,1},{1,0},{2,3},{3,2},{4,5},{5,4},{6,7},{7,6},{8,9},{9,8},{10,11... | collective-permute-start | bytes 768008 | tf_op jit(solution)/shard_map/ppermute | solution.py:147
  92.3 11.7 %all-to-all-start.1 = ((f16[8,2,32,512]{3,2,1,0:T(8,128)(2,1)}), f16[8,2,32,512]{3,2,1,0:T(8,128)(2,1)S(1)}, u32[]{:S(2)}, u32[]{:S(2)}) async-start(f16[8,2,32,512]{3,2,1,0:T(8,128)(2,1)} %convert_element_type.30), calls=%async_computation.1 | async-start | bytes 1048576 | tf_op jit(solution)/shard_map/all_to_all | solution.py:473

commit v2 on v1

v2 whole, which is shorter than its diff:
```python
import jax
import jax.numpy as jnp
from jax import lax
from jax.experimental import pallas as pl
from jax.experimental.pallas import tpu as pltpu
from jax.sharding import PartitionSpec as P


FINE_DIFF = 0.2
FINE_ADV = 0.3
COARSE_DIFF = 0.24
COARSE_ADV = 0.4

F32 = jnp.float32
LINK = jnp.float16
LANE = 128
SUB = 8
ROWS = 32
COLS = 4096
CHUNK = 512
WIDE = 640
PAD = COLS + 2 * LANE
NEAR = 40
FAR = 72
NDEV = 8
NCOARSE = 16
GROUP = 3
MIB = 1024 * 1024

VM = pl.BlockSpec(memory_space=pltpu.VMEM)
SM = pl.BlockSpec(memory_space=pltpu.SMEM)


def halo_tiles():
    return [(j, 1 if j <= 6 else (2 if j < 15 else 3)) for j in range(1, NCOARSE)]


def call(kernel, outs, args, scratch=(), flops=10_000_000, vmem=16, space=pltpu.VMEM):
    specs = [SM if a.dtype == jnp.int32 else pl.BlockSpec(memory_space=space) for a in args]
    nbytes = sum(a.size * a.dtype.itemsize for a in args)
    return pl.pallas_call(
        kernel,
        out_shape=outs,
        in_specs=specs,
        out_specs=jax.tree.map(lambda _: VM, outs),
        scratch_shapes=list(scratch),
        compiler_params=pltpu.CompilerParams(vmem_limit_bytes=vmem * MIB),
        cost_estimate=pl.CostEstimate(flops=flops, bytes_accessed=nbytes, transcendentals=0),
    )(*args)


def sub_iota(cols):
    return lax.broadcasted_iota(jnp.int32, (SUB, cols), 0)


def lane_iota(rows):
    return lax.broadcasted_iota(jnp.int32, (rows, LANE), 1)


def roll4(x):
    return pltpu.roll(x, 4, 0)


def up(x):
    return pltpu.roll(x, x.shape[0] - 1, 0)


def down(x):
    return pltpu.roll(x, 1, 0)


def east(x):
    return pltpu.roll(x, x.shape[1] - 1, 1)


def west(x):
    return pltpu.roll(x, 1, 1)


def pack_fine(guess, sources, velocity, out_a, out_b, guess_v, sources_v, velocity_v, sems):
    odd = lax.rem(lax.axis_index("space"), 2) == 1
    copies = [pltpu.make_async_copy(velocity.at[k], velocity_v.at[k], sems.at[k]) for k in range(4)]
    copies.append(pltpu.make_async_copy(guess, guess_v, sems.at[4]))
    copies.append(pltpu.make_async_copy(sources, sources_v, sems.at[5]))
    for copy in copies:
        copy.start()
    first, final = slice(0, SUB), slice(ROWS - SUB, ROWS)
    vt, vb = velocity_v.at[:, :, first, :], velocity_v.at[:, :, final, :]
    st, sb = sources_v.at[:, first, :], sources_v.at[:, final, :]
    gt, gb = guess_v.at[:, first, :], guess_v.at[:, final, :]
    sub = sub_iota(COLS)
    low = sub < 4

    def put(n, top, bottom):
        out_a[n * SUB : (n + 1) * SUB, :] = jnp.where(odd, top, bottom).astype(jnp.bfloat16)
        out_b[n * SUB : (n + 1) * SUB, :] = jnp.where(odd, bottom, top).astype(jnp.bfloat16)

    def pair(n, x0, y0, x3, y3):
        put(n, jnp.where(low, x0, roll4(y0)), jnp.where(low, roll4(x3), y3))

    for k in range(4):
        copies[k].wait()
        pair(k, *(ref[k, c].astype(F32) for ref in (vt, vb) for c in (0, 1)))
    copies[4].wait()
    pair(4, gt[1], gt[0], gb[1], gb[0])
    copies[5].wait()
    pair(5, *(ref[n].astype(F32) for ref in (st, sb) for n in (3, 7)))
    top, bottom = st[2].astype(F32), pltpu.roll(sb[2].astype(F32), 2, 0)
    for i, n in enumerate((1, 6, 5)):
        here = sub >= 2 * i + 2
        top = jnp.where(here, pltpu.roll(st[n].astype(F32), 2 * i + 2, 0), top)
        more = sb[n].astype(F32)
        more = pltpu.roll(more, 2 * i + 4, 0) if i < 2 else more
        bottom = jnp.where(here, more, bottom)
    put(6, top, bottom)


FINE_TILES = 7
COARSE_TILES = 17


def chunk_at(t):
    base = pl.multiple_of(t * CHUNK, LANE)
    left = pl.multiple_of(jnp.maximum(t * CHUNK - LANE, 0), LANE)
    right = pl.multiple_of(jnp.minimum(t * CHUNK + CHUNK, COLS - LANE), LANE)
    return base, left, right


def pack_coarse(velocity, out_a, out_b):
    odd = lax.rem(lax.axis_index("space"), 2) == 1
    sub = sub_iota(WIDE)
    wide = lambda k, c, r: velocity[k, c, r : r + SUB, :].astype(F32)

    def place(n, top, bottom):
        at = slice(n * SUB, (n + 1) * SUB)
        out_a[at, :] = jnp.where(odd, top, bottom).astype(jnp.bfloat16)
        out_b[at, :] = jnp.where(odd, bottom, top).astype(jnp.bfloat16)

    for k in range(4):
        for c in range(2):
            for i in range(2):
                place((k * 2 + c) * 2 + i, wide(k, c, 8 * i), wide(k, c, 24 - 8 * i))
    top = jnp.zeros((SUB, WIDE), F32)
    bottom = top
    for k in range(4):
        x, y = wide(k, 0, 16), wide(k, 0, 8)
        top = jnp.where(sub == k, pltpu.roll(x, k, 0) if k else x, top)
        bottom = jnp.where(sub == k, pltpu.roll(y, k + 1, 0), bottom)
    place(16, top, bottom)


def swap(buf_a, buf_b):
    count = lax.axis_size("space")
    pairs_b = [(i, i + 1) for i in range(1, count - 1, 2)]
    pairs_b = pairs_b + [(j, i) for i, j in pairs_b]
    pairs_a = [(i, i ^ 1) for i in range(count)]
    got_b = lax.ppermute(buf_b, "space", pairs_b)
    got_a = lax.ppermute(buf_a, "space", pairs_a)
    return got_a, got_b


MID = slice(LANE, PAD - LANE)


def fine_step(p, coef, l0, width):
    at = pl.multiple_of(l0, LANE)
    mid = pl.multiple_of(l0 + LANE, LANE)
    pc = p[:, pl.ds(mid, width)]
    out = (1.0 - 4.0 * FINE_DIFF) * pc
    out = out + up(coef(0, mid, width) * pc) + down(coef(1, mid, width) * pc)
    ge = coef(2, mid, width + LANE) * p[:, pl.ds(mid, width + LANE)]
    gw = coef(3, at, width + LANE) * p[:, pl.ds(at, width + LANE)]
    return out + east(ge)[:, :width] + west(gw)[:, LANE:]


def coefficients(c, v):
    half = 0.5 * FINE_ADV * v
    return ((2 * c, FINE_DIFF + half), (2 * c + 1, FINE_DIFF - half))


def relax_chains(t, snapshot, step, last, start, pa, pb):
    first = t * 8
    start(pa, "second")
    step(pa, pb, snapshot[first + 3], 3)
    step(pb, pa, snapshot[first + 2], 2)
    step(pa, pb, snapshot[first + 1], 1)
    last(pb, snapshot[first], 0, 0)
    start(pa, "sources")
    step(pa, pb, snapshot[first + 6], 6)
    step(pb, pa, snapshot[first + 5], 5)
    last(pa, snapshot[first + 4], 4, 1)
    start(pa, "first")
    before = jnp.maximum(first - 4, 0)
    step(pa, pb, snapshot[before + 3], None)
    step(pb, pa, snapshot[before + 2], None)
    step(pa, pb, snapshot[before + 1], None)
    last(pb, snapshot[before], None, 2)


def first_inner(snapshot, guess, sources, velocity, res, base, edge_coef, own_vel, coarse_a, coarse_b, coef, pa, pb):
    t = lax.axis_index("tm")
    inner = (t > 0).astype(F32)
    zero = jnp.zeros((ROWS, LANE), F32)
    for buf in (pa, pb):
        buf[:, :LANE] = zero
        buf[:, PAD - LANE :] = zero
    for n in range(4):
        res[n, :, :LANE] = zero
        res[n, :, PAD - LANE :] = zero
        for c in range(4):
            coef[n, c, :, :LANE] = zero
            coef[n, c, :, PAD - LANE :] = zero
            edge_coef[n, c, :, :LANE] = zero[:16]
            edge_coef[n, c, :, PAD - LANE :] = zero[:16]

    for k in range(4):

        def build(c, carry):
            for r in range(0, ROWS, SUB):
                half = (0.5 * FINE_ADV) * velocity[k, c, r : r + SUB, :].astype(F32)
                for o, value in ((0, FINE_DIFF + half), (1, FINE_DIFF - half)):
                    coef[k, 2 * c + o, r : r + SUB, MID] = value
                    if r == 0:
                        edge_coef[k, 2 * c + o, SUB:, MID] = value
                    if r == ROWS - SUB:
                        edge_coef[k, 2 * c + o, :SUB, MID] = value
            return carry

        lax.fori_loop(0, 2, build, 0)
    at, left, right = chunk_at(t)
    half_lanes = lane_iota(ROWS) < 64
    for k in range(4):
        for c in range(2):
            own_vel[k, c, :, :CHUNK] = velocity[k, c, :, pl.ds(at, CHUNK)]
            x, y = velocity[k, c, :, pl.ds(right, LANE)], velocity[k, c, :, pl.ds(left, LANE)]
            own_vel[k, c, :, CHUNK:] = jnp.where(half_lanes, x.astype(F32), y.astype(F32)).astype(jnp.bfloat16)
    pack_coarse(own_vel, coarse_a, coarse_b)
    width = 1024

    def run(src, snap, use):
        def go(i, carry):
            l0 = i * width
            own = fine_step(src, lambda c, o, w: coef[snap, c, :, pl.ds(o, w)], l0, width)
            use(own, pl.ds(pl.multiple_of(l0, LANE), width), pl.ds(pl.multiple_of(l0 + LANE, LANE), width))
            return carry

        lax.fori_loop(0, COLS // width, go, 0)

    def step(src, dst, snap, source):
        def use(own, at, to):
            if source is not None:
                own = own + sources[source, :, at].astype(F32)
            dst[:, to] = own
            res[3, :, to] = res[3, :, to] + own

        run(src, snap, use)

    def last(src, snap, source, n):
        def use(own, at, to):
            if source is not None:
                own = own + sources[source, :, at].astype(F32)
                base[n, :, at] = own
                own = own - guess[n, :, at]
            res[n, :, to] = own

        run(src, snap, use)

    def start(buf, what):
        if what == "second":
            buf[:, MID] = guess[1]
        elif what == "sources":
            buf[:, MID] = sources[7].astype(F32)
        else:
            buf[:, MID] = guess[0] * inner

    res[3, :, MID] = guess[0] + guess[1] + sources[7].astype(F32)
    relax_chains(t, snapshot, step, last, start, pa, pb)


EDGE = 24


def first_edges(snapshot, guess, sources, in_a, in_b, inner_res, inner_base, edge_coef, pay, base, halo_coef, s_halo, pa, pb, acc, res):
    t = lax.axis_index("tm")
    s = lax.axis_index("space")
    odd = lax.rem(s, 2) == 1
    sub = sub_iota(COLS)
    low = sub < 4
    has_above = (s > 0).astype(F32)
    has_below = (s < lax.axis_size("space") - 1).astype(F32)
    inner = (t > 0).astype(F32)

    def tile(n):
        a = in_a[n * SUB : (n + 1) * SUB, :].astype(F32)
        b = in_b[n * SUB : (n + 1) * SUB, :].astype(F32)
        return jnp.where(odd, b, a), jnp.where(odd, a, b)

    def halves(n):
        below, above = tile(n)
        return jnp.where(low, below, roll4(above)), jnp.where(low, roll4(below), above)

    zero = jnp.zeros((EDGE, LANE), F32)
    for buf in (pa, pb):
        buf[:, :LANE] = zero
        buf[:, PAD - LANE :] = zero
    for k in range(4):
        pair = halves(k)
        for c in range(2):
            for n, value in coefficients(c, pair[c]):
                halo_coef[k, n, :, :LANE] = zero[:SUB]
                halo_coef[k, n, :, PAD - LANE :] = zero[:SUB]
                halo_coef[k, n, :, MID] = value
    g1, g0 = halves(4)
    s_halo[0], s_halo[4] = halves(5)
    below, above = tile(6)
    for i in range(4):
        x = pltpu.roll(below, 8 - 2 * i, 0) if i else below
        y = pltpu.roll(above, 6 - 2 * i, 0) if i < 3 else above
        s_halo[(2, 1, 6, 5)[i]] = jnp.where(sub < 2, x, jnp.where(sub >= 6, y, 0.0))
    s_halo[3] = s_halo[0]
    s_halo[7] = s_halo[4]

    width = 1024
    sub_w = sub_iota(width)
    edge = jnp.where(sub_w < 4, has_below, has_above)

    def run(src, snap, use):
        def coef(c, o, w):
            at = pl.ds(o, w)
            return jnp.concatenate(
                [edge_coef[snap, c, :SUB, at], halo_coef[snap, c, :, at], edge_coef[snap, c, SUB:, at]], 0
            )

        def go(i, carry):
            l0 = i * width
            out = fine_step(src, coef, l0, width)
            use(out, pl.ds(pl.multiple_of(l0, LANE), width), pl.ds(pl.multiple_of(l0 + LANE, LANE), width))
            return carry

        lax.fori_loop(0, COLS // width, go, 0)

    def tiles_of(source, at):
        return sources[source, ROWS - SUB :, at].astype(F32), sources[source, :SUB, at].astype(F32)

    def step(src, dst, snap, source):
        def use(out, at, to):
            x, h, y = out[:SUB], out[SUB : 2 * SUB] * edge, out[2 * SUB :]
            if source is not None:
                more = tiles_of(source, at)
                x, y = x + more[0], y + more[1]
                h = h + s_halo[source, :, at]
            dst[:SUB, to] = x
            dst[SUB : 2 * SUB, to] = h
            dst[2 * SUB :, to] = y
            acc[:SUB, at] = acc[:SUB, at] + x
            acc[SUB:, at] = acc[SUB:, at] + y

        run(src, snap, use)

    def last(src, snap, source, n):
        def use(out, at, to):
            x, y = out[:SUB], out[2 * SUB :]
            if source is not None:
                more = tiles_of(source, at)
                x, y = x + more[0], y + more[1]
                lo = sub_w < 4
                base[n, ROWS - SUB :, at] = jnp.where(lo, inner_base[n, ROWS - SUB :, at], x)
                base[n, :SUB, at] = jnp.where(lo, y, inner_base[n, :SUB, at])
                x = x - guess[n, ROWS - SUB :, at]
                y = y - guess[n, :SUB, at]
            res[n, :SUB, to] = x
            res[n, SUB:, to] = y

        run(src, snap, use)

    def start(buf, what):
        if what == "second":
            x, h, y = guess[1, ROWS - SUB :, :], g1, guess[1, :SUB, :]
        elif what == "sources":
            x, y = tiles_of(7, slice(None))
            h = s_halo[7]
        else:
            x, h, y = guess[0, ROWS - SUB :, :] * inner, g0 * inner, guess[0, :SUB, :] * inner
        buf[:SUB, MID] = x
        buf[SUB : 2 * SUB, MID] = h
        buf[2 * SUB :, MID] = y

    x7, y7 = tiles_of(7, slice(None))
    acc[:SUB, :] = guess[0, ROWS - SUB :, :] + guess[1, ROWS - SUB :, :] + x7
    acc[SUB:, :] = guess[0, :SUB, :] + guess[1, :SUB, :] + y7
    for n in range(4):
        res[n, :, :LANE] = zero[:16]
        res[n, :, PAD - LANE :] = zero[:16]
    for n in range(2):
        base[n, SUB : ROWS - SUB, :] = inner_base[n, SUB : ROWS - SUB, :]
    relax_chains(t, snapshot, step, last, start, pa, pb)
    res[3, :, MID] = acc[...]

    half = lane_iota(SUB) < 64
    lo = sub_iota(LANE) < 4

    def value(n, r, at):
        own = inner_res[n, r : r + SUB, at : at + LANE]
        if r == 0:
            return jnp.where(lo, res[n, SUB:, at : at + LANE], own)
        if r == ROWS - SUB:
            return jnp.where(lo, own, res[n, :SUB, at : at + LANE])
        return own

    for n in range(4):
        for r in range(0, ROWS, SUB):
            for d in range(NDEV):
                at = LANE + d * CHUNK
                for l in range(4):
                    pay[d, pl.ds(piece(n, l) + r, SUB), :] = value(n, r, at + l * LANE)
                if n < 3:
                    right, left = value(n, r, at + CHUNK), value(n, r, at - LANE)
                    pay[d, pl.ds(piece(n, 4) + r, SUB), :] = jnp.where(half, right, left)


PIECES = 19


def piece(n, l):
    return (5 * n + l) * ROWS


def field_rows(got, t, n, r, count):
    return jnp.concatenate([got[t, pl.ds(piece(n, l) + r, count), :] for l in range(5)], 1)


def level_rows(got, j, r):
    t, u = divmod(j, 2)
    value = field_rows(got, t, u, r, SUB)
    if u == 1 and t + 1 < NDEV:
        value = value + field_rows(got, t + 1, 2, r, SUB)
    return value


def pack_residual(got, out_a, out_b):
    odd = lax.rem(lax.axis_index("space"), 2) == 1
    n = 0
    for j, count in halo_tiles():
        for i in range(count):
            top, bottom = level_rows(got, j, 8 * i), level_rows(got, j, 24 - 8 * i)
            out_a[n * SUB : (n + 1) * SUB, :] = jnp.where(odd, top, bottom)
            out_b[n * SUB : (n + 1) * SUB, :] = jnp.where(odd, bottom, top)
            n += 1


def coarse_solve(snapshot, got, velocity, far_a, far_b, got_a, got_b, back, near, vnear, vel, res, mask):
    t = lax.axis_index("tm")
    s = lax.axis_index("space")
    odd = lax.rem(s, 2) == 1
    has_above = (s > 0).astype(F32)
    has_below = (s < lax.axis_size("space") - 1).astype(F32)
    has_left = (t > 0).astype(F32)
    has_right = (t < lax.axis_size("tm") - 1).astype(F32)
    row = lax.broadcasted_iota(jnp.int32, (FAR, WIDE), 0)
    col = lax.broadcasted_iota(jnp.int32, (FAR, WIDE), 1)
    in_rows = jnp.where(row < ROWS, 1.0, jnp.where(row < 52, has_below, has_above))
    in_cols = jnp.where(col < CHUNK, 1.0, jnp.where(col < CHUNK + 64, has_right, has_left))
    mask[...] = in_rows * in_cols

    sub = sub_iota(LANE)
    low = sub < 4

    def tile(n, l):
        at = (slice(n * SUB, (n + 1) * SUB), slice(l * LANE, (l + 1) * LANE))
        a, b = far_a[at].astype(F32), far_b[at].astype(F32)
        return jnp.where(odd, b, a), jnp.where(odd, a, b)

    coarse = 0.5 * COARSE_ADV
    for k in range(4):
        for c in range(2):
            for l in range(5):
                lanes = slice(l * LANE, (l + 1) * LANE)
                own = velocity[k, c, :, lanes].astype(F32)
                q = (k * 2 + c) * 2
                below0, above0 = tile(q, l)
                below1, above1 = tile(q + 1, l)
                edge = jnp.zeros((SUB, LANE), F32)
                if c == 0:
                    below, above = tile(16, l)
                    shifted = pltpu.roll(below, SUB - k, 0) if k else below
                    edge = jnp.where(sub == 0, shifted, edge)
                    edge = jnp.where(sub == 7, pltpu.roll(above, 7 - k, 0), edge)
                vel[k, c, :ROWS, lanes] = coarse * own
                vel[k, c, 32:40, lanes] = coarse * below0
                vel[k, c, 40:48, lanes] = coarse * below1
                vel[k, c, 48:56, lanes] = coarse * edge
                vel[k, c, 56:64, lanes] = coarse * above1
                vel[k, c, 64:72, lanes] = coarse * above0
                vnear[k, c, :ROWS, lanes] = velocity[k, c, :, lanes]
                vnear[k, c, ROWS:, lanes] = jnp.where(low, below0, above0).astype(jnp.bfloat16)

    n = 0
    low_w = sub_iota(WIDE) < 4
    empty = jnp.zeros((SUB, WIDE), F32)
    for j, count in halo_tiles():
        tiles = []
        for _ in range(count):
            a, b = got_a[n * SUB : (n + 1) * SUB, :], got_b[n * SUB : (n + 1) * SUB, :]
            tiles.append((jnp.where(odd, b, a), jnp.where(odd, a, b)))
            n += 1
        res[j, 32:40, :] = tiles[0][0]
        res[j, 64:72, :] = tiles[0][1]
        res[j, 40:48, :] = tiles[1][0] if count > 1 else empty
        res[j, 56:64, :] = tiles[1][1] if count > 1 else empty
        res[j, 48:56, :] = jnp.where(low_w, *tiles[2]) if count > 2 else empty
    res[0, ROWS:, :] = jnp.zeros((FAR - ROWS, WIDE), F32)
    for j in range(NCOARSE):
        res[j, :ROWS, :] = field_rows(got, j // 2, j % 2, 0, ROWS)

    for l in range(4):
        at = pl.ds(piece(3, l), ROWS)
        total = got[0, at, :]
        for d in range(1, NDEV):
            total = total + got[d, at, :]
        near[0, :ROWS, l * LANE : (l + 1) * LANE] = total

    def send(j, p, e):
        back[j // 2, j % 2] = e[:ROWS, :CHUNK]
        if j:
            near[j, :ROWS, :] = p[:ROWS]
            near[j, ROWS:, :] = jnp.where(low_w, p[32:40], p[64:72])
        near[0, :ROWS, :CHUNK] = near[0, :ROWS, :CHUNK] + p[:ROWS, :CHUNK]

    p = res[NCOARSE - 1]
    send(NCOARSE - 1, p, jnp.zeros_like(p))
    for j in range(NCOARSE - 2, -1, -1):
        snap = snapshot[4 * j]
        ax, ay = vel[snap, 0], vel[snap, 1]
        u = COARSE_DIFF * p
        wx = ax * p
        wy = ay * p
        e = (1.0 - 4.0 * COARSE_DIFF) * p + up(u + wx) + down(u - wx) + east(u + wy) + west(u - wy)
        e = e * mask[...]
        if j % 2 == 1:
            head = e[:ROWS] + field_rows(got, j // 2 + 1, 2, 0, ROWS)
            e = jnp.concatenate([head, e[ROWS:]], 0)
        p = e + res[j]
        send(j, p, e)


def second_relax(snapshot, near, vnear, grad, acc, coef):
    t = lax.axis_index("tm")
    s = lax.axis_index("space")
    has_above = (s > 0).astype(F32)
    has_below = (s < lax.axis_size("space") - 1).astype(F32)
    has_left = (t > 0).astype(F32)
    has_right = (t < lax.axis_size("tm") - 1).astype(F32)
    row = lax.broadcasted_iota(jnp.int32, (NEAR, WIDE), 0)
    col = lax.broadcasted_iota(jnp.int32, (NEAR, WIDE), 1)
    keep = (
        jnp.where(row == 0, has_above, 1.0),
        jnp.where(row == ROWS - 1, has_below, 1.0),
        jnp.where(col == 0, has_left, 1.0),
        jnp.where(col == CHUNK - 1, has_right, 1.0),
    )
    for k in range(4):
        for n in range(4):
            v = (0.5 * FINE_ADV) * vnear[k, n // 2].astype(F32)
            coef[k, n] = keep[n] * (FINE_DIFF - v if n % 2 else FINE_DIFF + v)
    acc[...] = near[0, :ROWS, :CHUNK]

    def interval(j):
        p = near[j + 1]
        total = None
        for k in (3, 2, 1):
            snap = snapshot[4 * j + k]
            c = [coef[snap, n] for n in range(4)]
            p = (1.0 - 4.0 * FINE_DIFF) * p + up(c[0] * p) + down(c[1] * p) + east(c[2] * p) + west(c[3] * p)
            own = p[:ROWS, :CHUNK]
            total = own if total is None else total + own
        return total

    def group(i, carry):
        total = interval(GROUP * i)
        for n in range(1, GROUP):
            total = total + interval(GROUP * i + n)
        acc[...] = acc[...] + total
        return carry

    lax.fori_loop(0, (NCOARSE - 1) // GROUP, group, 0)
    grad[...] = acc[...] * (1.0 / 64.0)


def finish(base, got, out):
    for d in range(NDEV):
        at = slice(d * CHUNK, (d + 1) * CHUNK)
        for u in range(2):
            out[u, :, at] = base[u, :, at] + got[d, u]


def cycle(guess, sources, velocity, snapshot):
    shape = jax.ShapeDtypeStruct
    bf = jnp.bfloat16
    packed = shape((FINE_TILES * SUB, COLS), bf)
    local = [shape(x.shape, x.dtype) for x in (guess, sources, velocity)]
    guess, sources, velocity = (pltpu.with_memory_space_constraint(x, pltpu.MemorySpace.HBM) for x in (guess, sources, velocity))
    fine_a, fine_b, guess, sources, velocity = call(
        pack_fine,
        (packed, packed, *local),
        (guess, sources, velocity),
        (pltpu.SemaphoreType.DMA((6,)),),
        vmem=12,
        space=pltpu.MemorySpace.HBM,
    )
    in_a, in_b = swap(fine_a, fine_b)
    field = lambda rows: pltpu.VMEM((rows, PAD), F32)
    coarse_rows = shape((COARSE_TILES * SUB, WIDE), bf)
    inner_res, inner_base, edge_coef, own_vel, coarse_a, coarse_b = call(
        first_inner,
        (
            shape((4, ROWS, PAD), F32),
            shape((2, ROWS, COLS), F32),
            shape((4, 4, 16, PAD), F32),
            shape((4, 2, ROWS, WIDE), bf),
            coarse_rows,
            coarse_rows,
        ),
        (snapshot, guess, sources, velocity),
        (pltpu.VMEM((4, 4, ROWS, PAD), F32), field(ROWS), field(ROWS)),
        vmem=24,
        flops=200_000_000,
    )
    far_a, far_b = swap(coarse_a, coarse_b)
    pay, base = call(
        first_edges,
        (shape((NDEV, PIECES * ROWS, LANE), F32), shape((2, ROWS, COLS), F32)),
        (snapshot, guess, sources, in_a, in_b, inner_res, inner_base, edge_coef),
        (
            pltpu.VMEM((4, 4, SUB, PAD), F32),
            pltpu.VMEM((8, SUB, COLS), F32),
            field(EDGE),
            field(EDGE),
            pltpu.VMEM((16, COLS), F32),
            pltpu.VMEM((4, 16, PAD), F32),
        ),
        vmem=20,
    )
    got = lax.all_to_all(pay.astype(LINK), "tm", 0, 0, tiled=False).astype(F32)
    tiles = sum(count for _, count in halo_tiles())
    edges = shape((tiles * SUB, WIDE), F32)
    send_a, send_b = call(pack_residual, (edges, edges), (got,), vmem=12)
    got_a, got_b = swap(send_a.astype(LINK), send_b.astype(LINK))
    back, near, vnear = call(
        coarse_solve,
        (
            shape((NDEV, 2, ROWS, CHUNK), F32),
            shape((NCOARSE, NEAR, WIDE), F32),
            shape((4, 2, NEAR, WIDE), bf),
        ),
        (snapshot, got, own_vel, far_a, far_b, got_a.astype(F32), got_b.astype(F32)),
        (
            pltpu.VMEM((4, 2, FAR, WIDE), F32),
            pltpu.VMEM((NCOARSE, FAR, WIDE), F32),
            pltpu.VMEM((FAR, WIDE), F32),
        ),
        vmem=20,
    )
    returned = lax.all_to_all(back.astype(LINK), "tm", 0, 0, tiled=False)
    grad = call(
        second_relax,
        shape((ROWS, CHUNK), F32),
        (snapshot, near, vnear),
        (pltpu.VMEM((ROWS, CHUNK), F32), pltpu.VMEM((4, 4, NEAR, WIDE), F32)),
        vmem=8,
    )
    c_values = call(finish, shape((2, ROWS, COLS), F32), (base, returned.astype(F32)), vmem=8)
    return c_values, grad


def solution(mesh):
    in_specs = (P("tm", "space", None), P("tm", "space", None), P(None, None, "space", None), P())
    out_specs = (P("tm", "space", None), P("space", "tm"))
    return jax.shard_map(cycle, mesh=mesh, in_specs=in_specs, out_specs=out_specs, check_vma=False)
```

time: 108 us -> 85.6 us (0.79)
  the two profiles are of different devices: /device:TPU:129 before, /device:TPU:97 now
where the time goes in v2:
time: 85.6 us; the launch traced here: 85.3 us
  Pallas kernels  29.8 us (35%)
  blocking collectives  20.1 us (23%)
  starting transfers between devices  18.4 us (21%)
  waiting for transfers between devices  13.7 us (16%)
  other arithmetic  2.52 us (3%)
    pallas_call x7, Pallas kernels, call(): pl.pallas_call(kernel, out_shape=outs, in_specs=specs, out_specs=jax.tree...  29.8 us
    all_to_all x1, blocking collectives, cycle(): got = lax.all_to_all(pay.astype(LINK), 'tm', 0, 0, tiled=False).astype(F32)  20.1 us
    ppermute x3, starting transfers between devices, swap(): got_b = lax.ppermute(buf_b, 'space', pairs_b)  12.9 us
    ppermute x3, waiting for transfers between devices, swap(): got_b = lax.ppermute(buf_b, 'space', pairs_b)  10.5 us
    all_to_all x1, starting transfers between devices, cycle(): returned = lax.all_to_all(back.astype(LINK), 'tm', 0, 0, tiled=False)  4.15 us
    all_to_all x1, waiting for transfers between devices, cycle(): returned = lax.all_to_all(back.astype(LINK), 'tm', 0, 0, tiled=False)  3.14 us
  transfers between devices with their start and end apart: 7, of which 4 were waited for; matrix products, arithmetic and copies ran while one was open for 0% of the time, Pallas kernels for 17%

profile of v2, /device:TPU:97, one launch (start us, length us, event | category | flops | bytes accessed | tf_op | source)
XLA Modules:
  0.0 85.3 jit_solution(6414906379602378595)
XLA Ops:
  0.6 2.8 %shard_map.59 = (bf16[56,4096]{1,0:T(8,128)(2,1)S(1)}, bf16[56,4096]{1,0:T(8,128)(2,1)S(1)}, f32[2,32,4096]{2,1,0:T(8,128)S(1)}, bf16[8,32,4096]{2,1,0:T(8,128)(2,1)S(1)}, bf16[4,2,32,4096]{3,2,1,0:T(8,128)(2,1)S(1)}) custom-call(f32[2,32,4096]{2,1,0:T(8,128)} %guess.1, bf16[8,32,4096]{2,1,0:T(8,128)(2,1)} %sources.1, bf16[4,2,32,4096]{3,2,1,0:T(8,128)(2,1)} %velocity.1), custom_call_target="tpu_custom_call" | custom-call | flops 10000000 | bytes 5242880 | tf_op jit(solution)/shard_map/pallas_call | solution.py:41
  3.4 0.8 collective-permute-start
  4.2 4.6 %collective-permute-start.1 = (bf16[56,4096]{1,0:T(8,128)(2,1)S(1)}, bf16[56,4096]{1,0:T(8,128)(2,1)S(1)}, u32[]{:S(2)}, u32[]{:S(2)}) collective-permute-start(bf16[56,4096]{1,0:T(8,128)(2,1)S(1)} %get-tuple-element.23), channel_id=1, source_target_pairs={{1,2},{3,4},{5,6},{7,8},{9,10},{11,12},{13,14},{15,16},{17,18},{19... | collective-permute-start | bytes 1376264 | tf_op jit(solution)/shard_map/ppermute | solution.py:157
  8.7 8.8 %shard_map.60 = (f32[4,32,4352]{2,1,0:T(8,128)S(1)}, f32[2,32,4096]{2,1,0:T(8,128)S(1)}, f32[4,4,16,4352]{3,2,1,0:T(8,128)S(1)}, bf16[4,2,32,640]{3,2,1,0:T(8,12...) custom-call(s32[64]{0:T(128)S(1)} %copy-done, f32[2,32,4096]{2,1,0:T(8,128)S(1)} %get-tuple-element.20.guess, ...), custom_call_target="tpu_custom_call" | custom-call | flops 200000000 | bytes 5243136 | tf_op jit(solution)/shard_map/pallas_call | solution.py:41
  17.5 2.9 %collective-permute-done.1.in_b = bf16[56,4096]{1,0:T(8,128)(2,1)S(1)} collective-permute-done((bf16[56,4096]{1,0:T(8,128)(2,1)S(1)}, bf16[56,4096]{1,0:T(8,128)(2,1)S(1)}, u32[]{:S(2)}, u32[]{:S(2)}) %collective-permute-start.1) | collective-permute-done | bytes 458784 | tf_op jit(solution)/shard_map/ppermute | solution.py:157
  20.4 7.6 %shard_map.61 = (f32[8,608,128]{2,1,0:T(8,128)S(1)}, f32[2,32,4096]{2,1,0:T(8,128)S(1)}) custom-call(s32[64]{0:T(128)S(1)} %copy-done, f32[2,32,4096]{2,1,0:T(8,128)S(1)} %get-tuple-element.20.guess, bf16[8,32,4096]{2,1,0:T(8,128)(2,1)S(1)} %get-tuple-element.21.sources, bf16[56,4096]{1,0:T(8,128)(2,1)S(1)} %collective-permute-done.in_a, ...), custom_call_target="tpu_custom_call" | custom-call | flops 10000000 | bytes 11796736 | tf_op jit(solution)/shard_map/pallas_call | solution.py:41
  28.0 0.2 convert_element_type.24
  28.1 20.1 %all_to_all.10 = f16[8,608,128]{2,1,0:T(8,128)(2,1)S(1)} all-to-all(f16[8,608,128]{2,1,0:T(8,128)(2,1)S(1)} %convert_element_type.24), channel_id=1, replica_groups=mesh['tm'=8,'space'=32] {'tm'}, dimensions={0} | all-to-all | bytes 2490368 | tf_op jit(solution)/shard_map/all_to_all | solution.py:643
  48.2 0.2 convert_element_type.25.got
  48.4 0.1 shard_map.62
  48.5 6.1 %collective-permute-start.5 = (f16[200,640]{1,0:T(8,128)(2,1)S(1)}, f16[200,640]{1,0:T(8,128)(2,1)S(1)}, u32[]{:S(2)}, u32[]{:S(2)}) collective-permute-start(f16[200,640]{1,0:T(8,128)(2,1)S(1)} %convert_element_type.28), channel_id=1, source_target_pairs={{1,2},{3,4},{5,6},{7,8},{9,10},{11,12},{13,14},{15,16},{17,18},{19... | collective-permute-start | bytes 768008 | tf_op jit(solution)/shard_map/ppermute | solution.py:157
  54.6 0.1 collective-permute-start.4
  54.7 0.5 collective-permute-start.2
  55.2 2.3 %collective-permute-start.3 = (bf16[136,640]{1,0:T(8,128)(2,1)S(1)}, bf16[136,640]{1,0:T(8,128)(2,1)S(1)}, u32[]{:S(2)}, u32[]{:S(2)}) collective-permute-start(bf16[136,640]{1,0:T(8,128)(2,1)S(1)} %get-tuple-element.32), channel_id=1, source_target_pairs={{1,2},{3,4},{5,6},{7,8},{9,10},{11,12},{13,14},{15,16},{17,18},{19... | collective-permute-start | bytes 522248 | tf_op jit(solution)/shard_map/ppermute | solution.py:157
  57.6 2.3 %collective-permute-done.5 = f16[200,640]{1,0:T(8,128)(2,1)S(1)} collective-permute-done((f16[200,640]{1,0:T(8,128)(2,1)S(1)}, f16[200,640]{1,0:T(8,128)(2,1)S(1)}, u32[]{:S(2)}, u32[]{:S(2)}) %collective-permute-start.5) | collective-permute-done | bytes 256032 | tf_op jit(solution)/shard_map/ppermute | solution.py:157
  59.9 0.0 collective-permute-done.2.far_a
  59.9 5.4 %collective-permute-done.3.far_b = bf16[136,640]{1,0:T(8,128)(2,1)S(1)} collective-permute-done((bf16[136,640]{1,0:T(8,128)(2,1)S(1)}, bf16[136,640]{1,0:T(8,128)(2,1)S(1)}, u32[]{:S(2)}, u32[]{:S(2)}) %collective-permute-start.3) | collective-permute-done | bytes 174112 | tf_op jit(solution)/shard_map/ppermute | solution.py:157
  65.3 3.5 %shard_map.63 = (f32[8,2,32,512]{3,2,1,0:T(8,128)S(1)}, f32[16,40,640]{2,1,0:T(8,128)S(1)}, bf16[4,2,40,640]{3,2,1,0:T(8,128)(2,1)S(1)}) custom-call(s32[64]{0:T(128)S(1)} %copy-done, f32[8,608,128]{2,1,0:T(8,128)S(1)} %convert_element_type.25.got, bf16[4,2,32,640]{3,2,1,0:T(8,128)(2,1)S(1)} %get-tuple-element.30.velocity, ...), custom_call_target="tpu_custom_call" | custom-call | flops 10000000 | bytes 4190464 | tf_op jit(solution)/shard_map/pallas_call | solution.py:41
  68.8 0.9 %convert_element_type.30 = f16[8,2,32,512]{3,2,1,0:T(8,128)(2,1)} convert(f32[8,2,32,512]{3,2,1,0:T(8,128)S(1)} %get-tuple-element.35) | non-fusion elementwise | flops 262144 | bytes 1572864 | tf_op jit(solution)/shard_map/convert_element_type | solution.py:663
  69.7 4.1 %all-to-all-start.1 = ((f16[8,2,32,512]{3,2,1,0:T(8,128)(2,1)}), f16[8,2,32,512]{3,2,1,0:T(8,128)(2,1)}, u32[]{:S(2)}, u32[]{:S(2)}) async-start(f16[8,2,32,512]{3,2,1,0:T(8,128)(2,1)} %convert_element_type.30), calls=%async_computation.1 | async-start | bytes 1048576 | tf_op jit(solution)/shard_map/all_to_all | solution.py:663
  73.9 6.0 %shard_map.65 = f32[32,512]{1,0:T(8,128)} custom-call(s32[64]{0:T(128)S(1)} %copy-done, f32[16,40,640]{2,1,0:T(8,128)S(1)} %get-tuple-element.36.near, bf16[4,2,40,640]{3,2,1,0:T(8,128)(2,1)S(1)} %get-tuple-element.37.vnear), custom_call_target="tpu_custom_call" | custom-call | flops 10000000 | bytes 2048256 | tf_op jit(solution)/shard_map/pallas_call | solution.py:41
  79.9 3.1 %all-to-all-done.1 = f16[8,2,32,512]{3,2,1,0:T(8,128)(2,1)} async-done(((f16[8,2,32,512]{3,2,1,0:T(8,128)(2,1)}), f16[8,2,32,512]{3,2,1,0:T(8,128)(2,1)}, u32[]{:S(2)}, u32[]{:S(2)}) %all-to-all-start.1) | async-done | bytes 524320 | tf_op jit(solution)/shard_map/all_to_all | solution.py:663
  83.0 1.2 %convert_element_type.31.got = f32[8,2,32,512]{3,2,1,0:T(8,128)S(1)} convert(f16[8,2,32,512]{3,2,1,0:T(8,128)(2,1)} %all-to-all-done.1) | non-fusion elementwise | flops 262144 | bytes 1572864 | tf_op jit(solution)/shard_map/convert_element_type | solution.py:671
  84.2 1.1 %shard_map.64 = f32[2,32,4096]{2,1,0:T(8,128)} custom-call(f32[2,32,4096]{2,1,0:T(8,128)S(1)} %get-tuple-element.28.base, f32[8,2,32,512]{3,2,1,0:T(8,128)S(1)} %convert_element_type.31.got), custom_call_target="tpu_custom_call" | custom-call | flops 10000000 | bytes 2097152 | tf_op jit(solution)/shard_map/pallas_call | solution.py:41
  (8 shorter events, 0.1 us)
Async XLA Ops:
  0.6 8.1 %copy-start = (s32[64]{0:T(128)S(1)}, s32[64]{0:T(128)}, u32[]{:S(2)}) copy-start(s32[64]{0:T(128)} %snapshot.7) | copy-start | bytes 772
  3.4 14.1 %collective-permute-start = (bf16[56,4096]{1,0:T(8,128)(2,1)S(1)}, bf16[56,4096]{1,0:T(8,128)(2,1)S(1)}, u32[]{:S(2)}, u32[]{:S(2)}) collective-permute-start(bf16[56,4096]{1,0:T(8,128)(2,1)S(1)} %get-tuple-element.22), channel_id=1, source_target_pairs={{0,1},{1,0},{2,3},{3,2},{4,5},{5,4},{6,7},{7,6},{8,9},{9,8},{10,11... | collective-permute-start | bytes 1376264 | tf_op jit(solution)/shard_map/ppermute | solution.py:158
  4.2 16.2 %collective-permute-start.1 = (bf16[56,4096]{1,0:T(8,128)(2,1)S(1)}, bf16[56,4096]{1,0:T(8,128)(2,1)S(1)}, u32[]{:S(2)}, u32[]{:S(2)}) collective-permute-start(bf16[56,4096]{1,0:T(8,128)(2,1)S(1)} %get-tuple-element.23), channel_id=1, source_target_pairs={{1,2},{3,4},{5,6},{7,8},{9,10},{11,12},{13,14},{15,16},{17,18},{19... | collective-permute-start | bytes 1376264 | tf_op jit(solution)/shard_map/ppermute | solution.py:157
  48.5 11.3 %collective-permute-start.5 = (f16[200,640]{1,0:T(8,128)(2,1)S(1)}, f16[200,640]{1,0:T(8,128)(2,1)S(1)}, u32[]{:S(2)}, u32[]{:S(2)}) collective-permute-start(f16[200,640]{1,0:T(8,128)(2,1)S(1)} %convert_element_type.28), channel_id=1, source_target_pairs={{1,2},{3,4},{5,6},{7,8},{9,10},{11,12},{13,14},{15,16},{17,18},{19... | collective-permute-start | bytes 768008 | tf_op jit(solution)/shard_map/ppermute | solution.py:157
  54.6 5.2 %collective-permute-start.4 = (f16[200,640]{1,0:T(8,128)(2,1)S(1)}, f16[200,640]{1,0:T(8,128)(2,1)S(1)}, u32[]{:S(2)}, u32[]{:S(2)}) collective-permute-start(f16[200,640]{1,0:T(8,128)(2,1)S(1)} %convert_element_type.26), channel_id=1, source_target_pairs={{0,1},{1,0},{2,3},{3,2},{4,5},{5,4},{6,7},{7,6},{8,9},{9,8},{10,11... | collective-permute-start | bytes 768008 | tf_op jit(solution)/shard_map/ppermute | solution.py:158
  54.7 5.2 %collective-permute-start.2 = (bf16[136,640]{1,0:T(8,128)(2,1)S(1)}, bf16[136,640]{1,0:T(8,128)(2,1)S(1)}, u32[]{:S(2)}, u32[]{:S(2)}) collective-permute-start(bf16[136,640]{1,0:T(8,128)(2,1)S(1)} %get-tuple-element.31), channel_id=1, source_target_pairs={{0,1},{1,0},{2,3},{3,2},{4,5},{5,4},{6,7},{7,6},{8,9},{9,8},{10,11... | collective-permute-start | bytes 522248 | tf_op jit(solution)/shard_map/ppermute | solution.py:158
  55.2 10.1 %collective-permute-start.3 = (bf16[136,640]{1,0:T(8,128)(2,1)S(1)}, bf16[136,640]{1,0:T(8,128)(2,1)S(1)}, u32[]{:S(2)}, u32[]{:S(2)}) collective-permute-start(bf16[136,640]{1,0:T(8,128)(2,1)S(1)} %get-tuple-element.32), channel_id=1, source_target_pairs={{1,2},{3,4},{5,6},{7,8},{9,10},{11,12},{13,14},{15,16},{17,18},{19... | collective-permute-start | bytes 522248 | tf_op jit(solution)/shard_map/ppermute | solution.py:157
  69.7 13.3 %all-to-all-start.1 = ((f16[8,2,32,512]{3,2,1,0:T(8,128)(2,1)}), f16[8,2,32,512]{3,2,1,0:T(8,128)(2,1)}, u32[]{:S(2)}, u32[]{:S(2)}) async-start(f16[8,2,32,512]{3,2,1,0:T(8,128)(2,1)} %convert_element_type.30), calls=%async_computation.1 | async-start | bytes 1048576 | tf_op jit(solution)/shard_map/all_to_all | solution.py:663

commit v3 on v2

--- a/solution.py
+++ b/solution.py
@@ -31,8 +31,20 @@
 SM = pl.BlockSpec(memory_space=pltpu.SMEM)
 
 
-def halo_tiles():
-    return [(j, 1 if j <= 6 else (2 if j < 15 else 3)) for j in range(1, NCOARSE)]
+def halo_rows():
+    parts = []
+    for j in range(1, NCOARSE):
+        for i, left in enumerate(range(j + 2, 0, -SUB)):
+            parts.append((j, i, min(left, SUB)))
+    parts.sort(key=lambda part: (-part[2], part[0]))
+    tiles = []
+    while parts:
+        first = parts.pop(0)
+        fits = [part for part in parts if part[2] + first[2] <= SUB]
+        if fits:
+            parts.remove(fits[0])
+        tiles.append((first, *fits[:1]))
+    return tiles
 
 
 def call(kernel, outs, args, scratch=(), flops=10_000_000, vmem=16, space=pltpu.VMEM):
@@ -98,24 +110,29 @@
     def pair(n, x0, y0, x3, y3):
         put(n, jnp.where(low, x0, roll4(y0)), jnp.where(low, roll4(x3), y3))
 
-    for k in range(4):
-        copies[k].wait()
-        pair(k, *(ref[k, c].astype(F32) for ref in (vt, vb) for c in (0, 1)))
+    def turn(x, by):
+        return pltpu.roll(x, by, 0) if by % SUB else x
+
     copies[4].wait()
     pair(4, gt[1], gt[0], gb[1], gb[0])
     copies[5].wait()
-    pair(5, *(ref[n].astype(F32) for ref in (st, sb) for n in (3, 7)))
-    top, bottom = st[2].astype(F32), pltpu.roll(sb[2].astype(F32), 2, 0)
-    for i, n in enumerate((1, 6, 5)):
-        here = sub >= 2 * i + 2
-        top = jnp.where(here, pltpu.roll(st[n].astype(F32), 2 * i + 2, 0), top)
-        more = sb[n].astype(F32)
-        more = pltpu.roll(more, 2 * i + 4, 0) if i < 2 else more
-        bottom = jnp.where(here, more, bottom)
-    put(6, top, bottom)
-
-
-FINE_TILES = 7
+    for k in range(4):
+        copies[k].wait()
+        n, r = (2, 2, 6, 6)[k], k % 2
+        x0, y0, x3, y3 = (ref[k, c].astype(F32) for ref in (vt, vb) for c in (0, 1))
+        top = jnp.where(low, x0, roll4(y0))
+        bottom = jnp.where(low, roll4(x3), y3)
+        top = jnp.where(sub == 7, turn(st[n].astype(F32), 7 - r), top)
+        bottom = jnp.where(sub == 4, turn(sb[n].astype(F32), 6 - r), bottom)
+        put(k, top, bottom)
+    top = jnp.where(low, st[3].astype(F32), roll4(st[7].astype(F32)))
+    bottom = jnp.where(low, roll4(sb[3].astype(F32)), sb[7].astype(F32))
+    top = jnp.where(sub == 3, turn(st[1].astype(F32), 3), jnp.where(sub == 7, turn(st[5].astype(F32), 7), top))
+    bottom = jnp.where(sub == 0, turn(sb[1].astype(F32), 1), jnp.where(sub == 4, turn(sb[5].astype(F32), 5), bottom))
+    put(5, top, bottom)
+
+
+FINE_TILES = 6
 COARSE_TILES = 17
 
 
@@ -244,7 +261,7 @@
             use(own, pl.ds(pl.multiple_of(l0, LANE), width), pl.ds(pl.multiple_of(l0 + LANE, LANE), width))
             return carry
 
-        lax.fori_loop(0, COLS // width, go, 0)
+        lax.fori_loop(0, COLS // width, go, 0, unroll=True)
 
     def step(src, dst, snap, source):
         def use(own, at, to):
@@ -311,14 +328,18 @@
                 halo_coef[k, n, :, PAD - LANE :] = zero[:SUB]
                 halo_coef[k, n, :, MID] = value
     g1, g0 = halves(4)
-    s_halo[0], s_halo[4] = halves(5)
-    below, above = tile(6)
-    for i in range(4):
-        x = pltpu.roll(below, 8 - 2 * i, 0) if i else below
-        y = pltpu.roll(above, 6 - 2 * i, 0) if i < 3 else above
-        s_halo[(2, 1, 6, 5)[i]] = jnp.where(sub < 2, x, jnp.where(sub >= 6, y, 0.0))
-    s_halo[3] = s_halo[0]
-    s_halo[7] = s_halo[4]
+    s_halo[3], s_halo[7] = halves(5)
+
+    def turn(x, by):
+        return pltpu.roll(x, by, 0) if by % SUB else x
+
+    for n, k in ((2, 0), (6, 2)):
+        (t0, b0), (t1, b1) = tile(k), tile(k + 1)
+        value = jnp.where(sub == 0, turn(t0, 1), jnp.where(sub == 1, turn(t1, 2), 0.0))
+        s_halo[n] = jnp.where(sub == 6, turn(b0, 2), jnp.where(sub == 7, turn(b1, 3), value))
+    below, above = tile(5)
+    for n, x, y in ((1, 5, 7), (5, 1, 3)):
+        s_halo[n] = jnp.where(sub == 0, turn(below, x), jnp.where(sub == 7, turn(above, y), 0.0))
 
     width = 1024
     sub_w = sub_iota(width)
@@ -337,7 +358,7 @@
             use(out, pl.ds(pl.multiple_of(l0, LANE), width), pl.ds(pl.multiple_of(l0 + LANE, LANE), width))
             return carry
 
-        lax.fori_loop(0, COLS // width, go, 0)
+        lax.fori_loop(0, COLS // width, go, 0, unroll=True)
 
     def tiles_of(source, at):
         return sources[source, ROWS - SUB :, at].astype(F32), sources[source, :SUB, at].astype(F32)
@@ -439,13 +460,15 @@
 
 def pack_residual(got, out_a, out_b):
     odd = lax.rem(lax.axis_index("space"), 2) == 1
-    n = 0
-    for j, count in halo_tiles():
-        for i in range(count):
-            top, bottom = level_rows(got, j, 8 * i), level_rows(got, j, 24 - 8 * i)
-            out_a[n * SUB : (n + 1) * SUB, :] = jnp.where(odd, top, bottom)
-            out_b[n * SUB : (n + 1) * SUB, :] = jnp.where(odd, bottom, top)
-            n += 1
+    sub = sub_iota(WIDE)
+    for n, parts in enumerate(halo_rows()):
+        (j, i, a), rest = parts[0], parts[1:]
+        top, bottom = level_rows(got, j, SUB * i), level_rows(got, j, 24 - SUB * i)
+        for j, i, _ in rest:
+            top = jnp.where(sub < a, top, pltpu.roll(level_rows(got, j, SUB * i), a, 0))
+            bottom = jnp.where(sub >= SUB - a, bottom, pltpu.roll(level_rows(got, j, 24 - SUB * i), SUB - a, 0))
+        out_a[n * SUB : (n + 1) * SUB, :] = jnp.where(odd, top, bottom)
+        out_b[n * SUB : (n + 1) * SUB, :] = jnp.where(odd, bottom, top)
 
 
 def coarse_solve(snapshot, got, velocity, far_a, far_b, got_a, got_b, back, near, vnear, vel, res, mask):
@@ -494,20 +517,26 @@
                 vnear[k, c, :ROWS, lanes] = velocity[k, c, :, lanes]
                 vnear[k, c, ROWS:, lanes] = jnp.where(low, below0, above0).astype(jnp.bfloat16)
 
-    n = 0
     low_w = sub_iota(WIDE) < 4
     empty = jnp.zeros((SUB, WIDE), F32)
-    for j, count in halo_tiles():
-        tiles = []
-        for _ in range(count):
-            a, b = got_a[n * SUB : (n + 1) * SUB, :], got_b[n * SUB : (n + 1) * SUB, :]
-            tiles.append((jnp.where(odd, b, a), jnp.where(odd, a, b)))
-            n += 1
-        res[j, 32:40, :] = tiles[0][0]
-        res[j, 64:72, :] = tiles[0][1]
-        res[j, 40:48, :] = tiles[1][0] if count > 1 else empty
-        res[j, 56:64, :] = tiles[1][1] if count > 1 else empty
-        res[j, 48:56, :] = jnp.where(low_w, *tiles[2]) if count > 2 else empty
+    for j in range(1, NCOARSE):
+        if j + 2 <= SUB:
+            res[j, 40:48, :] = empty
+            res[j, 56:64, :] = empty
+        if j + 2 <= 2 * SUB:
+            res[j, 48:56, :] = empty
+    for n, parts in enumerate(halo_rows()):
+        a, b = got_a[n * SUB : (n + 1) * SUB, :], got_b[n * SUB : (n + 1) * SUB, :]
+        below, above = jnp.where(odd, b, a), jnp.where(odd, a, b)
+        for m, (j, i, _) in enumerate(parts):
+            if m:
+                used = parts[0][2]
+                below, above = pltpu.roll(below, SUB - used, 0), pltpu.roll(above, used, 0)
+            if i == 2:
+                res[j, 48:56, :] = jnp.where(low_w, below, above)
+            else:
+                res[j, 32 + SUB * i : 40 + SUB * i, :] = below
+                res[j, 64 - SUB * i : 72 - SUB * i, :] = above
     res[0, ROWS:, :] = jnp.zeros((FAR - ROWS, WIDE), F32)
     for j in range(NCOARSE):
         res[j, :ROWS, :] = field_rows(got, j // 2, j % 2, 0, ROWS)
@@ -641,7 +670,7 @@
         vmem=20,
     )
     got = lax.all_to_all(pay.astype(LINK), "tm", 0, 0, tiled=False).astype(F32)
-    tiles = sum(count for _, count in halo_tiles())
+    tiles = len(halo_rows())
     edges = shape((tiles * SUB, WIDE), F32)
     send_a, send_b = call(pack_residual, (edges, edges), (got,), vmem=12)
     got_a, got_b = swap(send_a.astype(LINK), send_b.astype(LINK))

time: 85.6 us -> 81.3 us (0.950)
  Pallas kernels: 29.8 us -> 24.7 us
  starting transfers between devices: 18.4 us -> 20.1 us
  waiting for transfers between devices: 13.7 us -> 12.4 us
    pallas_call x7, Pallas kernels: 29.8 us -> 24.7 us  [call(): pl.pallas_call(kernel, out_shape=outs, in_specs=specs, out_specs=jax.tree...]
    ppermute x3, starting transfers between devices: 12.9 us -> 14.6 us  [swap(): got_b = lax.ppermute(buf_b, 'space', pairs_b)]
    ppermute x3, waiting for transfers between devices: 10.5 us -> 9.25 us  [swap(): got_b = lax.ppermute(buf_b, 'space', pairs_b)]
  transfers between devices with their start and end apart: 7 -> 7, of which waited for: 4 -> 3; matrix products, arithmetic and copies ran while one was open for 0% -> 0% of each run, Pallas kernels for 17% -> 15%
where the time goes in v3:
time: 81.3 us; the launch traced here: 81 us
  Pallas kernels  24.7 us (30%)
  blocking collectives  20.5 us (25%)
  starting transfers between devices  20.1 us (25%)
  waiting for transfers between devices  12.4 us (15%)
  other arithmetic  2.5 us (3%)
    pallas_call x7, Pallas kernels, call(): pl.pallas_call(kernel, out_shape=outs, in_specs=specs, out_specs=jax.tree...  24.7 us
    all_to_all x1, blocking collectives, cycle(): got = lax.all_to_all(pay.astype(LINK), 'tm', 0, 0, tiled=False).astype(F32)  20.5 us
    ppermute x3, starting transfers between devices, swap(): got_b = lax.ppermute(buf_b, 'space', pairs_b)  14.6 us
    ppermute x3, waiting for transfers between devices, swap(): got_b = lax.ppermute(buf_b, 'space', pairs_b)  9.25 us
    all_to_all x1, starting transfers between devices, cycle(): returned = lax.all_to_all(back.astype(LINK), 'tm', 0, 0, tiled=False)  4.15 us
    all_to_all x1, waiting for transfers between devices, cycle(): returned = lax.all_to_all(back.astype(LINK), 'tm', 0, 0, tiled=False)  3.14 us
  transfers between devices with their start and end apart: 7, of which 3 were waited for; matrix products, arithmetic and copies ran while one was open for 0% of the time, Pallas kernels for 15%

profile of v3, /device:TPU:97, one launch (start us, length us, event | category | flops | bytes accessed | tf_op | source)
XLA Modules:
  0.0 81.0 jit_solution(15240949813248413988)
XLA Ops:
  0.6 3.0 %shard_map.59 = (bf16[48,4096]{1,0:T(8,128)(2,1)S(1)}, bf16[48,4096]{1,0:T(8,128)(2,1)S(1)}, f32[2,32,4096]{2,1,0:T(8,128)S(1)}, bf16[8,32,4096]{2,1,0:T(8,128)(2,1)S(1)}, bf16[4,2,32,4096]{3,2,1,0:T(8,128)(2,1)S(1)}) custom-call(f32[2,32,4096]{2,1,0:T(8,128)} %guess.1, bf16[8,32,4096]{2,1,0:T(8,128)(2,1)} %sources.1, bf16[4,2,32,4096]{3,2,1,0:T(8,128)(2,1)} %velocity.1), custom_call_target="tpu_custom_call" | custom-call | flops 10000000 | bytes 5242880 | tf_op jit(solution)/shard_map/pallas_call | solution.py:53
  3.7 0.8 collective-permute-start
  4.4 4.6 %collective-permute-start.1 = (bf16[48,4096]{1,0:T(8,128)(2,1)S(1)}, bf16[48,4096]{1,0:T(8,128)(2,1)S(1)}, u32[]{:S(2)}, u32[]{:S(2)}) collective-permute-start(bf16[48,4096]{1,0:T(8,128)(2,1)S(1)} %get-tuple-element.23), channel_id=1, source_target_pairs={{1,2},{3,4},{5,6},{7,8},{9,10},{11,12},{13,14},{15,16},{17,18},{19... | collective-permute-start | bytes 1179656 | tf_op jit(solution)/shard_map/ppermute | solution.py:174
  9.0 6.4 %shard_map.60 = (f32[4,32,4352]{2,1,0:T(8,128)S(1)}, f32[2,32,4096]{2,1,0:T(8,128)S(1)}, f32[4,4,16,4352]{3,2,1,0:T(8,128)S(1)}, bf16[4,2,32,640]{3,2,1,0:T(8,12...) custom-call(s32[64]{0:T(128)S(1)} %copy-done, f32[2,32,4096]{2,1,0:T(8,128)S(1)} %get-tuple-element.20.guess, ...), custom_call_target="tpu_custom_call" | custom-call | flops 200000000 | bytes 5243136 | tf_op jit(solution)/shard_map/pallas_call | solution.py:53
  15.4 3.8 %collective-permute-done.1.in_b = bf16[48,4096]{1,0:T(8,128)(2,1)S(1)} collective-permute-done((bf16[48,4096]{1,0:T(8,128)(2,1)S(1)}, bf16[48,4096]{1,0:T(8,128)(2,1)S(1)}, u32[]{:S(2)}, u32[]{:S(2)}) %collective-permute-start.1) | collective-permute-done | bytes 393248 | tf_op jit(solution)/shard_map/ppermute | solution.py:174
  19.2 4.5 %shard_map.61 = (f32[8,608,128]{2,1,0:T(8,128)S(1)}, f32[2,32,4096]{2,1,0:T(8,128)S(1)}) custom-call(s32[64]{0:T(128)S(1)} %copy-done, f32[2,32,4096]{2,1,0:T(8,128)S(1)} %get-tuple-element.20.guess, bf16[8,32,4096]{2,1,0:T(8,128)(2,1)S(1)} %get-tuple-element.21.sources, bf16[48,4096]{1,0:T(8,128)(2,1)S(1)} %collective-permute-done.in_a, ...), custom_call_target="tpu_custom_call" | custom-call | flops 10000000 | bytes 11665664 | tf_op jit(solution)/shard_map/pallas_call | solution.py:53
  23.8 0.2 convert_element_type.24
  24.0 20.5 %all_to_all.10 = f16[8,608,128]{2,1,0:T(8,128)(2,1)S(1)} all-to-all(f16[8,608,128]{2,1,0:T(8,128)(2,1)S(1)} %convert_element_type.24), channel_id=1, replica_groups=mesh['tm'=8,'space'=32] {'tm'}, dimensions={0} | all-to-all | bytes 2490368 | tf_op jit(solution)/shard_map/all_to_all | solution.py:672
  44.5 0.2 convert_element_type.25.got
  44.7 0.1 shard_map.62
  44.8 5.5 %collective-permute-start.5 = (f16[152,640]{1,0:T(8,128)(2,1)S(1)}, f16[152,640]{1,0:T(8,128)(2,1)S(1)}, u32[]{:S(2)}, u32[]{:S(2)}) collective-permute-start(f16[152,640]{1,0:T(8,128)(2,1)S(1)} %convert_element_type.28), channel_id=1, source_target_pairs={{1,2},{3,4},{5,6},{7,8},{9,10},{11,12},{13,14},{15,16},{17,18},{19... | collective-permute-start | bytes 583688 | tf_op jit(solution)/shard_map/ppermute | solution.py:174
  50.3 0.1 collective-permute-start.4
  50.4 0.5 collective-permute-start.2
  50.9 4.5 %collective-permute-start.3 = (bf16[136,640]{1,0:T(8,128)(2,1)S(1)}, bf16[136,640]{1,0:T(8,128)(2,1)S(1)}, u32[]{:S(2)}, u32[]{:S(2)}) collective-permute-start(bf16[136,640]{1,0:T(8,128)(2,1)S(1)} %get-tuple-element.32), channel_id=1, source_target_pairs={{1,2},{3,4},{5,6},{7,8},{9,10},{11,12},{13,14},{15,16},{17,18},{19... | collective-permute-start | bytes 522248 | tf_op jit(solution)/shard_map/ppermute | solution.py:174
  55.5 0.0 collective-permute-done.5
  55.5 0.0 collective-permute-done.4
  55.6 5.5 %collective-permute-done.3.far_b = bf16[136,640]{1,0:T(8,128)(2,1)S(1)} collective-permute-done((bf16[136,640]{1,0:T(8,128)(2,1)S(1)}, bf16[136,640]{1,0:T(8,128)(2,1)S(1)}, u32[]{:S(2)}, u32[]{:S(2)}) %collective-permute-start.3) | collective-permute-done | bytes 174112 | tf_op jit(solution)/shard_map/ppermute | solution.py:174
  61.0 3.5 %shard_map.63 = (f32[8,2,32,512]{3,2,1,0:T(8,128)S(1)}, f32[16,40,640]{2,1,0:T(8,128)S(1)}, bf16[4,2,40,640]{3,2,1,0:T(8,128)(2,1)S(1)}) custom-call(s32[64]{0:T(128)S(1)} %copy-done, f32[8,608,128]{2,1,0:T(8,128)S(1)} %convert_element_type.25.got, bf16[4,2,32,640]{3,2,1,0:T(8,128)(2,1)S(1)} %get-tuple-element.30.velocity, ...), custom_call_target="tpu_custom_call" | custom-call | flops 10000000 | bytes 3944704 | tf_op jit(solution)/shard_map/pallas_call | solution.py:53
  64.5 0.9 %convert_element_type.30 = f16[8,2,32,512]{3,2,1,0:T(8,128)(2,1)} convert(f32[8,2,32,512]{3,2,1,0:T(8,128)S(1)} %get-tuple-element.35) | non-fusion elementwise | flops 262144 | bytes 1572864 | tf_op jit(solution)/shard_map/convert_element_type | solution.py:692
  65.4 4.1 %all-to-all-start.1 = ((f16[8,2,32,512]{3,2,1,0:T(8,128)(2,1)}), f16[8,2,32,512]{3,2,1,0:T(8,128)(2,1)}, u32[]{:S(2)}, u32[]{:S(2)}) async-start(f16[8,2,32,512]{3,2,1,0:T(8,128)(2,1)} %convert_element_type.30), calls=%async_computation.1 | async-start | bytes 1048576 | tf_op jit(solution)/shard_map/all_to_all | solution.py:692
  69.6 6.0 %shard_map.65 = f32[32,512]{1,0:T(8,128)} custom-call(s32[64]{0:T(128)S(1)} %copy-done, f32[16,40,640]{2,1,0:T(8,128)S(1)} %get-tuple-element.36.near, bf16[4,2,40,640]{3,2,1,0:T(8,128)(2,1)S(1)} %get-tuple-element.37.vnear), custom_call_target="tpu_custom_call" | custom-call | flops 10000000 | bytes 2048256 | tf_op jit(solution)/shard_map/pallas_call | solution.py:53
  75.6 3.1 %all-to-all-done.1 = f16[8,2,32,512]{3,2,1,0:T(8,128)(2,1)} async-done(((f16[8,2,32,512]{3,2,1,0:T(8,128)(2,1)}), f16[8,2,32,512]{3,2,1,0:T(8,128)(2,1)}, u32[]{:S(2)}, u32[]{:S(2)}) %all-to-all-start.1) | async-done | bytes 524320 | tf_op jit(solution)/shard_map/all_to_all | solution.py:692
  78.7 1.2 %convert_element_type.31.got = f32[8,2,32,512]{3,2,1,0:T(8,128)S(1)} convert(f16[8,2,32,512]{3,2,1,0:T(8,128)(2,1)} %all-to-all-done.1) | non-fusion elementwise | flops 262144 | bytes 1572864 | tf_op jit(solution)/shard_map/convert_element_type | solution.py:700
  79.9 1.1 %shard_map.64 = f32[2,32,4096]{2,1,0:T(8,128)} custom-call(f32[2,32,4096]{2,1,0:T(8,128)S(1)} %get-tuple-element.28.base, f32[8,2,32,512]{3,2,1,0:T(8,128)S(1)} %convert_element_type.31.got), custom_call_target="tpu_custom_call" | custom-call | flops 10000000 | bytes 2097152 | tf_op jit(solution)/shard_map/pallas_call | solution.py:53
  (8 shorter events, 0.1 us)
Async XLA Ops:
  0.6 8.4 %copy-start = (s32[64]{0:T(128)S(1)}, s32[64]{0:T(128)}, u32[]{:S(2)}) copy-start(s32[64]{0:T(128)} %snapshot.7) | copy-start | bytes 772
  3.7 11.8 %collective-permute-start = (bf16[48,4096]{1,0:T(8,128)(2,1)S(1)}, bf16[48,4096]{1,0:T(8,128)(2,1)S(1)}, u32[]{:S(2)}, u32[]{:S(2)}) collective-permute-start(bf16[48,4096]{1,0:T(8,128)(2,1)S(1)} %get-tuple-element.22), channel_id=1, source_target_pairs={{0,1},{1,0},{2,3},{3,2},{4,5},{5,4},{6,7},{7,6},{8,9},{9,8},{10,11... | collective-permute-start | bytes 1179656 | tf_op jit(solution)/shard_map/ppermute | solution.py:175
  4.4 14.8 %collective-permute-start.1 = (bf16[48,4096]{1,0:T(8,128)(2,1)S(1)}, bf16[48,4096]{1,0:T(8,128)(2,1)S(1)}, u32[]{:S(2)}, u32[]{:S(2)}) collective-permute-start(bf16[48,4096]{1,0:T(8,128)(2,1)S(1)} %get-tuple-element.23), channel_id=1, source_target_pairs={{1,2},{3,4},{5,6},{7,8},{9,10},{11,12},{13,14},{15,16},{17,18},{19... | collective-permute-start | bytes 1179656 | tf_op jit(solution)/shard_map/ppermute | solution.py:174
  44.8 10.7 %collective-permute-start.5 = (f16[152,640]{1,0:T(8,128)(2,1)S(1)}, f16[152,640]{1,0:T(8,128)(2,1)S(1)}, u32[]{:S(2)}, u32[]{:S(2)}) collective-permute-start(f16[152,640]{1,0:T(8,128)(2,1)S(1)} %convert_element_type.28), channel_id=1, source_target_pairs={{1,2},{3,4},{5,6},{7,8},{9,10},{11,12},{13,14},{15,16},{17,18},{19... | collective-permute-start | bytes 583688 | tf_op jit(solution)/shard_map/ppermute | solution.py:174
  50.3 5.2 %collective-permute-start.4 = (f16[152,640]{1,0:T(8,128)(2,1)S(1)}, f16[152,640]{1,0:T(8,128)(2,1)S(1)}, u32[]{:S(2)}, u32[]{:S(2)}) collective-permute-start(f16[152,640]{1,0:T(8,128)(2,1)S(1)} %convert_element_type.26), channel_id=1, source_target_pairs={{0,1},{1,0},{2,3},{3,2},{4,5},{5,4},{6,7},{7,6},{8,9},{9,8},{10,11... | collective-permute-start | bytes 583688 | tf_op jit(solution)/shard_map/ppermute | solution.py:175
  50.4 5.1 %collective-permute-start.2 = (bf16[136,640]{1,0:T(8,128)(2,1)S(1)}, bf16[136,640]{1,0:T(8,128)(2,1)S(1)}, u32[]{:S(2)}, u32[]{:S(2)}) collective-permute-start(bf16[136,640]{1,0:T(8,128)(2,1)S(1)} %get-tuple-element.31), channel_id=1, source_target_pairs={{0,1},{1,0},{2,3},{3,2},{4,5},{5,4},{6,7},{7,6},{8,9},{9,8},{10,11... | collective-permute-start | bytes 522248 | tf_op jit(solution)/shard_map/ppermute | solution.py:175
  50.9 10.1 %collective-permute-start.3 = (bf16[136,640]{1,0:T(8,128)(2,1)S(1)}, bf16[136,640]{1,0:T(8,128)(2,1)S(1)}, u32[]{:S(2)}, u32[]{:S(2)}) collective-permute-start(bf16[136,640]{1,0:T(8,128)(2,1)S(1)} %get-tuple-element.32), channel_id=1, source_target_pairs={{1,2},{3,4},{5,6},{7,8},{9,10},{11,12},{13,14},{15,16},{17,18},{19... | collective-permute-start | bytes 522248 | tf_op jit(solution)/shard_map/ppermute | solution.py:174
  65.4 13.3 %all-to-all-start.1 = ((f16[8,2,32,512]{3,2,1,0:T(8,128)(2,1)}), f16[8,2,32,512]{3,2,1,0:T(8,128)(2,1)}, u32[]{:S(2)}, u32[]{:S(2)}) async-start(f16[8,2,32,512]{3,2,1,0:T(8,128)(2,1)} %convert_element_type.30), calls=%async_computation.1 | async-start | bytes 1048576 | tf_op jit(solution)/shard_map/all_to_all | solution.py:692

commit v4 on v3

--- a/solution.py
+++ b/solution.py
@@ -417,7 +417,7 @@
     relax_chains(t, snapshot, step, last, start, pa, pb)
     res[3, :, MID] = acc[...]
 
-    half = lane_iota(SUB) < 64
+    lane = lane_iota(SUB)
     lo = sub_iota(LANE) < 4
 
     def value(n, r, at):
@@ -434,20 +434,44 @@
                 at = LANE + d * CHUNK
                 for l in range(4):
                     pay[d, pl.ds(piece(n, l) + r, SUB), :] = value(n, r, at + l * LANE)
-                if n < 3:
-                    right, left = value(n, r, at + CHUNK), value(n, r, at - LANE)
-                    pay[d, pl.ds(piece(n, 4) + r, SUB), :] = jnp.where(half, right, left)
-
-
-PIECES = 19
+
+    def turn(x, by):
+        return pltpu.roll(x, by % LANE, 1) if by % LANE else x
+
+    for d in range(NDEV):
+        at = LANE + d * CHUNK
+        parts = []
+        for q in range(12):
+            n, r = divmod(q, 4)
+            slot = 2 * HALO * (q % 3)
+            parts.append(turn(value(n, SUB * r, at + CHUNK), slot))
+            parts.append(turn(value(n, SUB * r, at - LANE), slot + 2 * HALO))
+        for m in range(4):
+            packed = parts[6 * m + 5]
+            for k in range(4, -1, -1):
+                packed = jnp.where(lane < HALO * (k + 1), parts[6 * m + k], packed)
+            pay[d, pl.ds(piece(4, 0) + SUB * m, SUB), :] = packed
+
+
+HALO = 20
+PIECES = 17
 
 
 def piece(n, l):
-    return (5 * n + l) * ROWS
+    return (4 * n + l) * ROWS
+
+
+def halo_columns(got, t, n, r):
+    m, slot = divmod(4 * n + r // SUB, 3)
+    x = got[t, pl.ds(piece(4, 0) + SUB * m, SUB), :]
+    right = pltpu.roll(x, LANE - 2 * HALO * slot, 1) if slot else x
+    left = pltpu.roll(x, (2 * LANE - 2 * HALO * (slot + 1)) % LANE, 1)
+    return jnp.where(lane_iota(SUB) < 64, right, left)
 
 
 def field_rows(got, t, n, r, count):
-    return jnp.concatenate([got[t, pl.ds(piece(n, l) + r, count), :] for l in range(5)], 1)
+    last = jnp.concatenate([halo_columns(got, t, n, r + i) for i in range(0, count, SUB)], 0)
+    return jnp.concatenate([*(got[t, pl.ds(piece(n, l) + r, count), :] for l in range(4)), last], 1)
 
 
 def level_rows(got, j, r):

time: 81.3 us -> 80.2 us (0.986)
  blocking collectives: 20.5 us -> 19.2 us
    all_to_all x1, blocking collectives: 20.5 us -> 19.2 us  [cycle(): got = lax.all_to_all(pay.astype(LINK), 'tm', 0, 0, tiled=False).astype(F32)]
  transfers between devices with their start and end apart: 7 -> 7, of which waited for: 3 -> 3; matrix products, arithmetic and copies ran while one was open for 0% -> 0% of each run, Pallas kernels for 15% -> 16%
where the time goes in v4:
time: 80.2 us; the launch traced here: 79.9 us
  Pallas kernels  24.9 us (31%)
  starting transfers between devices  20.1 us (25%)
  blocking collectives  19.2 us (24%)
  waiting for transfers between devices  12.4 us (15%)
  other arithmetic  2.46 us (3%)
  between operations  0.81 us (1%)
    pallas_call x7, Pallas kernels, call(): pl.pallas_call(kernel, out_shape=outs, in_specs=specs, out_specs=jax.tree...  24.9 us
    all_to_all x1, blocking collectives, cycle(): got = lax.all_to_all(pay.astype(LINK), 'tm', 0, 0, tiled=False).astype(F32)  19.2 us
    ppermute x3, starting transfers between devices, swap(): got_b = lax.ppermute(buf_b, 'space', pairs_b)  14.6 us
    ppermute x3, waiting for transfers between devices, swap(): got_b = lax.ppermute(buf_b, 'space', pairs_b)  9.25 us
    all_to_all x1, starting transfers between devices, cycle(): returned = lax.all_to_all(back.astype(LINK), 'tm', 0, 0, tiled=False)  4.15 us
    all_to_all x1, waiting for transfers between devices, cycle(): returned = lax.all_to_all(back.astype(LINK), 'tm', 0, 0, tiled=False)  3.14 us
  transfers between devices with their start and end apart: 7, of which 3 were waited for; matrix products, arithmetic and copies ran while one was open for 0% of the time, Pallas kernels for 16%

profile of v4, /device:TPU:97, one launch (start us, length us, event | category | flops | bytes accessed | tf_op | source)
XLA Modules:
  0.0 79.9 jit_solution(5280718357070919697)
XLA Ops:
  0.6 3.0 %shard_map.59 = (bf16[48,4096]{1,0:T(8,128)(2,1)S(1)}, bf16[48,4096]{1,0:T(8,128)(2,1)S(1)}, f32[2,32,4096]{2,1,0:T(8,128)S(1)}, bf16[8,32,4096]{2,1,0:T(8,128)(2,1)S(1)}, bf16[4,2,32,4096]{3,2,1,0:T(8,128)(2,1)S(1)}) custom-call(f32[2,32,4096]{2,1,0:T(8,128)} %guess.1, bf16[8,32,4096]{2,1,0:T(8,128)(2,1)} %sources.1, bf16[4,2,32,4096]{3,2,1,0:T(8,128)(2,1)} %velocity.1), custom_call_target="tpu_custom_call" | custom-call | flops 10000000 | bytes 5242880 | tf_op jit(solution)/shard_map/pallas_call | solution.py:53
  3.7 0.8 collective-permute-start
  4.4 4.6 %collective-permute-start.1 = (bf16[48,4096]{1,0:T(8,128)(2,1)S(1)}, bf16[48,4096]{1,0:T(8,128)(2,1)S(1)}, u32[]{:S(2)}, u32[]{:S(2)}) collective-permute-start(bf16[48,4096]{1,0:T(8,128)(2,1)S(1)} %get-tuple-element.23), channel_id=1, source_target_pairs={{1,2},{3,4},{5,6},{7,8},{9,10},{11,12},{13,14},{15,16},{17,18},{19... | collective-permute-start | bytes 1179656 | tf_op jit(solution)/shard_map/ppermute | solution.py:174
  9.0 6.4 %shard_map.60 = (f32[4,32,4352]{2,1,0:T(8,128)S(1)}, f32[2,32,4096]{2,1,0:T(8,128)S(1)}, f32[4,4,16,4352]{3,2,1,0:T(8,128)S(1)}, bf16[4,2,32,640]{3,2,1,0:T(8,12...) custom-call(s32[64]{0:T(128)S(1)} %copy-done, f32[2,32,4096]{2,1,0:T(8,128)S(1)} %get-tuple-element.20.guess, ...), custom_call_target="tpu_custom_call" | custom-call | flops 200000000 | bytes 5243136 | tf_op jit(solution)/shard_map/pallas_call | solution.py:53
  15.4 0.0 collective-permute-done.in_a
  15.4 3.8 %collective-permute-done.1.in_b = bf16[48,4096]{1,0:T(8,128)(2,1)S(1)} collective-permute-done((bf16[48,4096]{1,0:T(8,128)(2,1)S(1)}, bf16[48,4096]{1,0:T(8,128)(2,1)S(1)}, u32[]{:S(2)}, u32[]{:S(2)}) %collective-permute-start.1) | collective-permute-done | bytes 393248 | tf_op jit(solution)/shard_map/ppermute | solution.py:174
  19.2 4.7 %shard_map.61 = (f32[8,544,128]{2,1,0:T(8,128)S(1)}, f32[2,32,4096]{2,1,0:T(8,128)S(1)}) custom-call(s32[64]{0:T(128)S(1)} %copy-done, f32[2,32,4096]{2,1,0:T(8,128)S(1)} %get-tuple-element.20.guess, bf16[8,32,4096]{2,1,0:T(8,128)(2,1)S(1)} %get-tuple-element.21.sources, bf16[48,4096]{1,0:T(8,128)(2,1)S(1)} %collective-permute-done.in_a, ...), custom_call_target="tpu_custom_call" | custom-call | flops 10000000 | bytes 11665664 | tf_op jit(solution)/shard_map/pallas_call | solution.py:53
  23.9 0.1 convert_element_type.24
  24.1 19.2 %all_to_all.10 = f16[8,544,128]{2,1,0:T(8,128)(2,1)S(1)} all-to-all(f16[8,544,128]{2,1,0:T(8,128)(2,1)S(1)} %convert_element_type.24), channel_id=1, replica_groups=mesh['tm'=8,'space'=32] {'tm'}, dimensions={0} | all-to-all | bytes 2228224 | tf_op jit(solution)/shard_map/all_to_all | solution.py:696
  43.3 0.1 convert_element_type.25.got
  43.5 0.2 shard_map.62
  43.7 5.5 %collective-permute-start.5 = (f16[152,640]{1,0:T(8,128)(2,1)S(1)}, f16[152,640]{1,0:T(8,128)(2,1)S(1)}, u32[]{:S(2)}, u32[]{:S(2)}) collective-permute-start(f16[152,640]{1,0:T(8,128)(2,1)S(1)} %convert_element_type.28), channel_id=1, source_target_pairs={{1,2},{3,4},{5,6},{7,8},{9,10},{11,12},{13,14},{15,16},{17,18},{19... | collective-permute-start | bytes 583688 | tf_op jit(solution)/shard_map/ppermute | solution.py:174
  49.2 0.1 collective-permute-start.4
  49.3 0.5 collective-permute-start.2
  49.8 4.5 %collective-permute-start.3 = (bf16[136,640]{1,0:T(8,128)(2,1)S(1)}, bf16[136,640]{1,0:T(8,128)(2,1)S(1)}, u32[]{:S(2)}, u32[]{:S(2)}) collective-permute-start(bf16[136,640]{1,0:T(8,128)(2,1)S(1)} %get-tuple-element.32), channel_id=1, source_target_pairs={{1,2},{3,4},{5,6},{7,8},{9,10},{11,12},{13,14},{15,16},{17,18},{19... | collective-permute-start | bytes 522248 | tf_op jit(solution)/shard_map/ppermute | solution.py:174
  54.4 0.0 collective-permute-done.5
  54.5 5.5 %collective-permute-done.3.far_b = bf16[136,640]{1,0:T(8,128)(2,1)S(1)} collective-permute-done((bf16[136,640]{1,0:T(8,128)(2,1)S(1)}, bf16[136,640]{1,0:T(8,128)(2,1)S(1)}, u32[]{:S(2)}, u32[]{:S(2)}) %collective-permute-start.3) | collective-permute-done | bytes 174112 | tf_op jit(solution)/shard_map/ppermute | solution.py:174
  59.9 3.5 %shard_map.63 = (f32[8,2,32,512]{3,2,1,0:T(8,128)S(1)}, f32[16,40,640]{2,1,0:T(8,128)S(1)}, bf16[4,2,40,640]{3,2,1,0:T(8,128)(2,1)S(1)}) custom-call(s32[64]{0:T(128)S(1)} %copy-done, f32[8,544,128]{2,1,0:T(8,128)S(1)} %convert_element_type.25.got, bf16[4,2,32,640]{3,2,1,0:T(8,128)(2,1)S(1)} %get-tuple-element.30.velocity, ...), custom_call_target="tpu_custom_call" | custom-call | flops 10000000 | bytes 3682560 | tf_op jit(solution)/shard_map/pallas_call | solution.py:53
  63.4 0.9 %convert_element_type.30 = f16[8,2,32,512]{3,2,1,0:T(8,128)(2,1)} convert(f32[8,2,32,512]{3,2,1,0:T(8,128)S(1)} %get-tuple-element.35) | non-fusion elementwise | flops 262144 | bytes 1572864 | tf_op jit(solution)/shard_map/convert_element_type | solution.py:716
  64.3 4.1 %all-to-all-start.1 = ((f16[8,2,32,512]{3,2,1,0:T(8,128)(2,1)}), f16[8,2,32,512]{3,2,1,0:T(8,128)(2,1)}, u32[]{:S(2)}, u32[]{:S(2)}) async-start(f16[8,2,32,512]{3,2,1,0:T(8,128)(2,1)} %convert_element_type.30), calls=%async_computation.1 | async-start | bytes 1048576 | tf_op jit(solution)/shard_map/all_to_all | solution.py:716
  68.5 6.0 %shard_map.65 = f32[32,512]{1,0:T(8,128)} custom-call(s32[64]{0:T(128)S(1)} %copy-done, f32[16,40,640]{2,1,0:T(8,128)S(1)} %get-tuple-element.36.near, bf16[4,2,40,640]{3,2,1,0:T(8,128)(2,1)S(1)} %get-tuple-element.37.vnear), custom_call_target="tpu_custom_call" | custom-call | flops 10000000 | bytes 2048256 | tf_op jit(solution)/shard_map/pallas_call | solution.py:53
  74.5 3.1 %all-to-all-done.1 = f16[8,2,32,512]{3,2,1,0:T(8,128)(2,1)} async-done(((f16[8,2,32,512]{3,2,1,0:T(8,128)(2,1)}), f16[8,2,32,512]{3,2,1,0:T(8,128)(2,1)}, u32[]{:S(2)}, u32[]{:S(2)}) %all-to-all-start.1) | async-done | bytes 524320 | tf_op jit(solution)/shard_map/all_to_all | solution.py:716
  77.6 1.2 %convert_element_type.31.got = f32[8,2,32,512]{3,2,1,0:T(8,128)S(1)} convert(f16[8,2,32,512]{3,2,1,0:T(8,128)(2,1)} %all-to-all-done.1) | non-fusion elementwise | flops 262144 | bytes 1572864 | tf_op jit(solution)/shard_map/convert_element_type | solution.py:724
  78.8 1.1 %shard_map.64 = f32[2,32,4096]{2,1,0:T(8,128)} custom-call(f32[2,32,4096]{2,1,0:T(8,128)S(1)} %get-tuple-element.28.base, f32[8,2,32,512]{3,2,1,0:T(8,128)S(1)} %convert_element_type.31.got), custom_call_target="tpu_custom_call" | custom-call | flops 10000000 | bytes 2097152 | tf_op jit(solution)/shard_map/pallas_call | solution.py:53
  (8 shorter events, 0.1 us)
Async XLA Ops:
  0.6 8.4 %copy-start = (s32[64]{0:T(128)S(1)}, s32[64]{0:T(128)}, u32[]{:S(2)}) copy-start(s32[64]{0:T(128)} %snapshot.7) | copy-start | bytes 772
  3.7 11.8 %collective-permute-start = (bf16[48,4096]{1,0:T(8,128)(2,1)S(1)}, bf16[48,4096]{1,0:T(8,128)(2,1)S(1)}, u32[]{:S(2)}, u32[]{:S(2)}) collective-permute-start(bf16[48,4096]{1,0:T(8,128)(2,1)S(1)} %get-tuple-element.22), channel_id=1, source_target_pairs={{0,1},{1,0},{2,3},{3,2},{4,5},{5,4},{6,7},{7,6},{8,9},{9,8},{10,11... | collective-permute-start | bytes 1179656 | tf_op jit(solution)/shard_map/ppermute | solution.py:175
  4.4 14.8 %collective-permute-start.1 = (bf16[48,4096]{1,0:T(8,128)(2,1)S(1)}, bf16[48,4096]{1,0:T(8,128)(2,1)S(1)}, u32[]{:S(2)}, u32[]{:S(2)}) collective-permute-start(bf16[48,4096]{1,0:T(8,128)(2,1)S(1)} %get-tuple-element.23), channel_id=1, source_target_pairs={{1,2},{3,4},{5,6},{7,8},{9,10},{11,12},{13,14},{15,16},{17,18},{19... | collective-permute-start | bytes 1179656 | tf_op jit(solution)/shard_map/ppermute | solution.py:174
  43.7 10.7 %collective-permute-start.5 = (f16[152,640]{1,0:T(8,128)(2,1)S(1)}, f16[152,640]{1,0:T(8,128)(2,1)S(1)}, u32[]{:S(2)}, u32[]{:S(2)}) collective-permute-start(f16[152,640]{1,0:T(8,128)(2,1)S(1)} %convert_element_type.28), channel_id=1, source_target_pairs={{1,2},{3,4},{5,6},{7,8},{9,10},{11,12},{13,14},{15,16},{17,18},{19... | collective-permute-start | bytes 583688 | tf_op jit(solution)/shard_map/ppermute | solution.py:174
  49.2 5.2 %collective-permute-start.4 = (f16[152,640]{1,0:T(8,128)(2,1)S(1)}, f16[152,640]{1,0:T(8,128)(2,1)S(1)}, u32[]{:S(2)}, u32[]{:S(2)}) collective-permute-start(f16[152,640]{1,0:T(8,128)(2,1)S(1)} %convert_element_type.26), channel_id=1, source_target_pairs={{0,1},{1,0},{2,3},{3,2},{4,5},{5,4},{6,7},{7,6},{8,9},{9,8},{10,11... | collective-permute-start | bytes 583688 | tf_op jit(solution)/shard_map/ppermute | solution.py:175
  49.3 5.1 %collective-permute-start.2 = (bf16[136,640]{1,0:T(8,128)(2,1)S(1)}, bf16[136,640]{1,0:T(8,128)(2,1)S(1)}, u32[]{:S(2)}, u32[]{:S(2)}) collective-permute-start(bf16[136,640]{1,0:T(8,128)(2,1)S(1)} %get-tuple-element.31), channel_id=1, source_target_pairs={{0,1},{1,0},{2,3},{3,2},{4,5},{5,4},{6,7},{7,6},{8,9},{9,8},{10,11... | collective-permute-start | bytes 522248 | tf_op jit(solution)/shard_map/ppermute | solution.py:175
  49.8 10.1 %collective-permute-start.3 = (bf16[136,640]{1,0:T(8,128)(2,1)S(1)}, bf16[136,640]{1,0:T(8,128)(2,1)S(1)}, u32[]{:S(2)}, u32[]{:S(2)}) collective-permute-start(bf16[136,640]{1,0:T(8,128)(2,1)S(1)} %get-tuple-element.32), channel_id=1, source_target_pairs={{1,2},{3,4},{5,6},{7,8},{9,10},{11,12},{13,14},{15,16},{17,18},{19... | collective-permute-start | bytes 522248 | tf_op jit(solution)/shard_map/ppermute | solution.py:174
  64.3 13.3 %all-to-all-start.1 = ((f16[8,2,32,512]{3,2,1,0:T(8,128)(2,1)}), f16[8,2,32,512]{3,2,1,0:T(8,128)(2,1)}, u32[]{:S(2)}, u32[]{:S(2)}) async-start(f16[8,2,32,512]{3,2,1,0:T(8,128)(2,1)} %convert_element_type.30), calls=%async_computation.1 | async-start | bytes 1048576 | tf_op jit(solution)/shard_map/all_to_all | solution.py:716

commit v5 on v4

--- a/solution.py
+++ b/solution.py
@@ -93,7 +93,7 @@
     odd = lax.rem(lax.axis_index("space"), 2) == 1
     copies = [pltpu.make_async_copy(velocity.at[k], velocity_v.at[k], sems.at[k]) for k in range(4)]
     copies.append(pltpu.make_async_copy(guess, guess_v, sems.at[4]))
-    copies.append(pltpu.make_async_copy(sources, sources_v, sems.at[5]))
+    copies += [pltpu.make_async_copy(sources.at[n], sources_v.at[n], sems.at[5 + n]) for n in range(8)]
     for copy in copies:
         copy.start()
     first, final = slice(0, SUB), slice(ROWS - SUB, ROWS)
@@ -115,7 +115,8 @@
 
     copies[4].wait()
     pair(4, gt[1], gt[0], gb[1], gb[0])
-    copies[5].wait()
+    for copy in copies[5:]:
+        copy.wait()
     for k in range(4):
         copies[k].wait()
         n, r = (2, 2, 6, 6)[k], k % 2
@@ -576,23 +577,31 @@
         back[j // 2, j % 2] = e[:ROWS, :CHUNK]
         if j:
             near[j, :ROWS, :] = p[:ROWS]
-            near[j, ROWS:, :] = jnp.where(low_w, p[32:40], p[64:72])
+            near[j, ROWS:, :] = jnp.where(low_w, p[32:40], p[p.shape[0] - SUB :])
         near[0, :ROWS, :CHUNK] = near[0, :ROWS, :CHUNK] + p[:ROWS, :CHUNK]
 
     p = res[NCOARSE - 1]
     send(NCOARSE - 1, p, jnp.zeros_like(p))
+
+    def cut(x):
+        return jnp.concatenate([x[:40], x[64:72]], 0)
+
     for j in range(NCOARSE - 2, -1, -1):
+        fit = cut if j <= 5 else lambda x: x
+        if j == 5:
+            p = cut(p)
         snap = snapshot[4 * j]
-        ax, ay = vel[snap, 0], vel[snap, 1]
+        ax, ay = fit(vel.at[snap, 0]), fit(vel.at[snap, 1])
+        ax, ay = ax[...], ay[...]
         u = COARSE_DIFF * p
         wx = ax * p
         wy = ay * p
         e = (1.0 - 4.0 * COARSE_DIFF) * p + up(u + wx) + down(u - wx) + east(u + wy) + west(u - wy)
-        e = e * mask[...]
+        e = e * fit(mask)[...]
         if j % 2 == 1:
             head = e[:ROWS] + field_rows(got, j // 2 + 1, 2, 0, ROWS)
             e = jnp.concatenate([head, e[ROWS:]], 0)
-        p = e + res[j]
+        p = e + fit(res.at[j])[...]
         send(j, p, e)
 
 
@@ -656,7 +665,7 @@
         pack_fine,
         (packed, packed, *local),
         (guess, sources, velocity),
-        (pltpu.SemaphoreType.DMA((6,)),),
+        (pltpu.SemaphoreType.DMA((13,)),),
         vmem=12,
         space=pltpu.MemorySpace.HBM,
     )

time: 80.2 us -> 79.9 us (level)
  no operation moved by 1% of the time
where the time goes in v5:
time: 79.9 us; the launch traced here: 79.6 us
  Pallas kernels  24.6 us (31%)
  starting transfers between devices  20.1 us (25%)
  blocking collectives  19.2 us (24%)
  waiting for transfers between devices  12.4 us (16%)
  other arithmetic  2.46 us (3%)
  between operations  0.81 us (1%)
    pallas_call x7, Pallas kernels, call(): pl.pallas_call(kernel, out_shape=outs, in_specs=specs, out_specs=jax.tree...  24.6 us
    all_to_all x1, blocking collectives, cycle(): got = lax.all_to_all(pay.astype(LINK), 'tm', 0, 0, tiled=False).astype(F32)  19.2 us
    ppermute x3, starting transfers between devices, swap(): got_b = lax.ppermute(buf_b, 'space', pairs_b)  14.6 us
    ppermute x3, waiting for transfers between devices, swap(): got_b = lax.ppermute(buf_b, 'space', pairs_b)  9.25 us
    all_to_all x1, starting transfers between devices, cycle(): returned = lax.all_to_all(back.astype(LINK), 'tm', 0, 0, tiled=False)  4.15 us
    all_to_all x1, waiting for transfers between devices, cycle(): returned = lax.all_to_all(back.astype(LINK), 'tm', 0, 0, tiled=False)  3.14 us
  transfers between devices with their start and end apart: 7, of which 3 were waited for; matrix products, arithmetic and copies ran while one was open for 0% of the time, Pallas kernels for 16%

profile of v5, /device:TPU:97, one launch (start us, length us, event | category | flops | bytes accessed | tf_op | source)
XLA Modules:
  0.0 79.6 jit_solution(13663200077145732518)
XLA Ops:
  0.6 3.0 %shard_map.59 = (bf16[48,4096]{1,0:T(8,128)(2,1)S(1)}, bf16[48,4096]{1,0:T(8,128)(2,1)S(1)}, f32[2,32,4096]{2,1,0:T(8,128)S(1)}, bf16[8,32,4096]{2,1,0:T(8,128)(2,1)S(1)}, bf16[4,2,32,4096]{3,2,1,0:T(8,128)(2,1)S(1)}) custom-call(f32[2,32,4096]{2,1,0:T(8,128)} %guess.1, bf16[8,32,4096]{2,1,0:T(8,128)(2,1)} %sources.1, bf16[4,2,32,4096]{3,2,1,0:T(8,128)(2,1)} %velocity.1), custom_call_target="tpu_custom_call" | custom-call | flops 10000000 | bytes 5242880 | tf_op jit(solution)/shard_map/pallas_call | solution.py:53
  3.6 0.8 collective-permute-start
  4.4 4.6 %collective-permute-start.1 = (bf16[48,4096]{1,0:T(8,128)(2,1)S(1)}, bf16[48,4096]{1,0:T(8,128)(2,1)S(1)}, u32[]{:S(2)}, u32[]{:S(2)}) collective-permute-start(bf16[48,4096]{1,0:T(8,128)(2,1)S(1)} %get-tuple-element.23), channel_id=1, source_target_pairs={{1,2},{3,4},{5,6},{7,8},{9,10},{11,12},{13,14},{15,16},{17,18},{19... | collective-permute-start | bytes 1179656 | tf_op jit(solution)/shard_map/ppermute | solution.py:175
  8.9 6.4 %shard_map.60 = (f32[4,32,4352]{2,1,0:T(8,128)S(1)}, f32[2,32,4096]{2,1,0:T(8,128)S(1)}, f32[4,4,16,4352]{3,2,1,0:T(8,128)S(1)}, bf16[4,2,32,640]{3,2,1,0:T(8,12...) custom-call(s32[64]{0:T(128)S(1)} %copy-done, f32[2,32,4096]{2,1,0:T(8,128)S(1)} %get-tuple-element.20.guess, ...), custom_call_target="tpu_custom_call" | custom-call | flops 200000000 | bytes 5243136 | tf_op jit(solution)/shard_map/pallas_call | solution.py:53
  15.4 3.8 %collective-permute-done.1.in_b = bf16[48,4096]{1,0:T(8,128)(2,1)S(1)} collective-permute-done((bf16[48,4096]{1,0:T(8,128)(2,1)S(1)}, bf16[48,4096]{1,0:T(8,128)(2,1)S(1)}, u32[]{:S(2)}, u32[]{:S(2)}) %collective-permute-start.1) | collective-permute-done | bytes 393248 | tf_op jit(solution)/shard_map/ppermute | solution.py:175
  19.2 4.7 %shard_map.61 = (f32[8,544,128]{2,1,0:T(8,128)S(1)}, f32[2,32,4096]{2,1,0:T(8,128)S(1)}) custom-call(s32[64]{0:T(128)S(1)} %copy-done, f32[2,32,4096]{2,1,0:T(8,128)S(1)} %get-tuple-element.20.guess, bf16[8,32,4096]{2,1,0:T(8,128)(2,1)S(1)} %get-tuple-element.21.sources, bf16[48,4096]{1,0:T(8,128)(2,1)S(1)} %collective-permute-done.in_a, ...), custom_call_target="tpu_custom_call" | custom-call | flops 10000000 | bytes 11665664 | tf_op jit(solution)/shard_map/pallas_call | solution.py:53
  23.9 0.1 convert_element_type.24
  24.0 19.2 %all_to_all.10 = f16[8,544,128]{2,1,0:T(8,128)(2,1)S(1)} all-to-all(f16[8,544,128]{2,1,0:T(8,128)(2,1)S(1)} %convert_element_type.24), channel_id=1, replica_groups=mesh['tm'=8,'space'=32] {'tm'}, dimensions={0} | all-to-all | bytes 2228224 | tf_op jit(solution)/shard_map/all_to_all | solution.py:705
  43.3 0.1 convert_element_type.25.got
  43.4 0.2 shard_map.62
  43.6 5.5 %collective-permute-start.5 = (f16[152,640]{1,0:T(8,128)(2,1)S(1)}, f16[152,640]{1,0:T(8,128)(2,1)S(1)}, u32[]{:S(2)}, u32[]{:S(2)}) collective-permute-start(f16[152,640]{1,0:T(8,128)(2,1)S(1)} %convert_element_type.28), channel_id=1, source_target_pairs={{1,2},{3,4},{5,6},{7,8},{9,10},{11,12},{13,14},{15,16},{17,18},{19... | collective-permute-start | bytes 583688 | tf_op jit(solution)/shard_map/ppermute | solution.py:175
  49.2 0.1 collective-permute-start.4
  49.3 0.5 collective-permute-start.2
  49.8 4.5 %collective-permute-start.3 = (bf16[136,640]{1,0:T(8,128)(2,1)S(1)}, bf16[136,640]{1,0:T(8,128)(2,1)S(1)}, u32[]{:S(2)}, u32[]{:S(2)}) collective-permute-start(bf16[136,640]{1,0:T(8,128)(2,1)S(1)} %get-tuple-element.32), channel_id=1, source_target_pairs={{1,2},{3,4},{5,6},{7,8},{9,10},{11,12},{13,14},{15,16},{17,18},{19... | collective-permute-start | bytes 522248 | tf_op jit(solution)/shard_map/ppermute | solution.py:175
  54.3 0.0 collective-permute-done.5
  54.3 0.0 collective-permute-done.4
  54.4 5.5 %collective-permute-done.3.far_b = bf16[136,640]{1,0:T(8,128)(2,1)S(1)} collective-permute-done((bf16[136,640]{1,0:T(8,128)(2,1)S(1)}, bf16[136,640]{1,0:T(8,128)(2,1)S(1)}, u32[]{:S(2)}, u32[]{:S(2)}) %collective-permute-start.3) | collective-permute-done | bytes 174112 | tf_op jit(solution)/shard_map/ppermute | solution.py:175
  59.9 3.2 %shard_map.63 = (f32[8,2,32,512]{3,2,1,0:T(8,128)S(1)}, f32[16,40,640]{2,1,0:T(8,128)S(1)}, bf16[4,2,40,640]{3,2,1,0:T(8,128)(2,1)S(1)}) custom-call(s32[64]{0:T(128)S(1)} %copy-done, f32[8,544,128]{2,1,0:T(8,128)S(1)} %convert_element_type.25.got, bf16[4,2,32,640]{3,2,1,0:T(8,128)(2,1)S(1)} %get-tuple-element.30.velocity, ...), custom_call_target="tpu_custom_call" | custom-call | flops 10000000 | bytes 3682560 | tf_op jit(solution)/shard_map/pallas_call | solution.py:53
  63.1 0.9 %convert_element_type.30 = f16[8,2,32,512]{3,2,1,0:T(8,128)(2,1)} convert(f32[8,2,32,512]{3,2,1,0:T(8,128)S(1)} %get-tuple-element.35) | non-fusion elementwise | flops 262144 | bytes 1572864 | tf_op jit(solution)/shard_map/convert_element_type | solution.py:725
  64.0 4.1 %all-to-all-start.1 = ((f16[8,2,32,512]{3,2,1,0:T(8,128)(2,1)}), f16[8,2,32,512]{3,2,1,0:T(8,128)(2,1)}, u32[]{:S(2)}, u32[]{:S(2)}) async-start(f16[8,2,32,512]{3,2,1,0:T(8,128)(2,1)} %convert_element_type.30), calls=%async_computation.1 | async-start | bytes 1048576 | tf_op jit(solution)/shard_map/all_to_all | solution.py:725
  68.2 6.0 %shard_map.65 = f32[32,512]{1,0:T(8,128)} custom-call(s32[64]{0:T(128)S(1)} %copy-done, f32[16,40,640]{2,1,0:T(8,128)S(1)} %get-tuple-element.36.near, bf16[4,2,40,640]{3,2,1,0:T(8,128)(2,1)S(1)} %get-tuple-element.37.vnear), custom_call_target="tpu_custom_call" | custom-call | flops 10000000 | bytes 2048256 | tf_op jit(solution)/shard_map/pallas_call | solution.py:53
  74.2 3.1 %all-to-all-done.1 = f16[8,2,32,512]{3,2,1,0:T(8,128)(2,1)} async-done(((f16[8,2,32,512]{3,2,1,0:T(8,128)(2,1)}), f16[8,2,32,512]{3,2,1,0:T(8,128)(2,1)}, u32[]{:S(2)}, u32[]{:S(2)}) %all-to-all-start.1) | async-done | bytes 524320 | tf_op jit(solution)/shard_map/all_to_all | solution.py:725
  77.3 1.2 %convert_element_type.31.got = f32[8,2,32,512]{3,2,1,0:T(8,128)S(1)} convert(f16[8,2,32,512]{3,2,1,0:T(8,128)(2,1)} %all-to-all-done.1) | non-fusion elementwise | flops 262144 | bytes 1572864 | tf_op jit(solution)/shard_map/convert_element_type | solution.py:733
  78.5 1.1 %shard_map.64 = f32[2,32,4096]{2,1,0:T(8,128)} custom-call(f32[2,32,4096]{2,1,0:T(8,128)S(1)} %get-tuple-element.28.base, f32[8,2,32,512]{3,2,1,0:T(8,128)S(1)} %convert_element_type.31.got), custom_call_target="tpu_custom_call" | custom-call | flops 10000000 | bytes 2097152 | tf_op jit(solution)/shard_map/pallas_call | solution.py:53
  (8 shorter events, 0.1 us)
Async XLA Ops:
  0.6 8.3 %copy-start = (s32[64]{0:T(128)S(1)}, s32[64]{0:T(128)}, u32[]{:S(2)}) copy-start(s32[64]{0:T(128)} %snapshot.7) | copy-start | bytes 772
  3.6 11.8 %collective-permute-start = (bf16[48,4096]{1,0:T(8,128)(2,1)S(1)}, bf16[48,4096]{1,0:T(8,128)(2,1)S(1)}, u32[]{:S(2)}, u32[]{:S(2)}) collective-permute-start(bf16[48,4096]{1,0:T(8,128)(2,1)S(1)} %get-tuple-element.22), channel_id=1, source_target_pairs={{0,1},{1,0},{2,3},{3,2},{4,5},{5,4},{6,7},{7,6},{8,9},{9,8},{10,11... | collective-permute-start | bytes 1179656 | tf_op jit(solution)/shard_map/ppermute | solution.py:176
  4.4 14.8 %collective-permute-start.1 = (bf16[48,4096]{1,0:T(8,128)(2,1)S(1)}, bf16[48,4096]{1,0:T(8,128)(2,1)S(1)}, u32[]{:S(2)}, u32[]{:S(2)}) collective-permute-start(bf16[48,4096]{1,0:T(8,128)(2,1)S(1)} %get-tuple-element.23), channel_id=1, source_target_pairs={{1,2},{3,4},{5,6},{7,8},{9,10},{11,12},{13,14},{15,16},{17,18},{19... | collective-permute-start | bytes 1179656 | tf_op jit(solution)/shard_map/ppermute | solution.py:175
  43.6 10.7 %collective-permute-start.5 = (f16[152,640]{1,0:T(8,128)(2,1)S(1)}, f16[152,640]{1,0:T(8,128)(2,1)S(1)}, u32[]{:S(2)}, u32[]{:S(2)}) collective-permute-start(f16[152,640]{1,0:T(8,128)(2,1)S(1)} %convert_element_type.28), channel_id=1, source_target_pairs={{1,2},{3,4},{5,6},{7,8},{9,10},{11,12},{13,14},{15,16},{17,18},{19... | collective-permute-start | bytes 583688 | tf_op jit(solution)/shard_map/ppermute | solution.py:175
  49.2 5.2 %collective-permute-start.4 = (f16[152,640]{1,0:T(8,128)(2,1)S(1)}, f16[152,640]{1,0:T(8,128)(2,1)S(1)}, u32[]{:S(2)}, u32[]{:S(2)}) collective-permute-start(f16[152,640]{1,0:T(8,128)(2,1)S(1)} %convert_element_type.26), channel_id=1, source_target_pairs={{0,1},{1,0},{2,3},{3,2},{4,5},{5,4},{6,7},{7,6},{8,9},{9,8},{10,11... | collective-permute-start | bytes 583688 | tf_op jit(solution)/shard_map/ppermute | solution.py:176
  49.3 5.1 %collective-permute-start.2 = (bf16[136,640]{1,0:T(8,128)(2,1)S(1)}, bf16[136,640]{1,0:T(8,128)(2,1)S(1)}, u32[]{:S(2)}, u32[]{:S(2)}) collective-permute-start(bf16[136,640]{1,0:T(8,128)(2,1)S(1)} %get-tuple-element.31), channel_id=1, source_target_pairs={{0,1},{1,0},{2,3},{3,2},{4,5},{5,4},{6,7},{7,6},{8,9},{9,8},{10,11... | collective-permute-start | bytes 522248 | tf_op jit(solution)/shard_map/ppermute | solution.py:176
  49.8 10.1 %collective-permute-start.3 = (bf16[136,640]{1,0:T(8,128)(2,1)S(1)}, bf16[136,640]{1,0:T(8,128)(2,1)S(1)}, u32[]{:S(2)}, u32[]{:S(2)}) collective-permute-start(bf16[136,640]{1,0:T(8,128)(2,1)S(1)} %get-tuple-element.32), channel_id=1, source_target_pairs={{1,2},{3,4},{5,6},{7,8},{9,10},{11,12},{13,14},{15,16},{17,18},{19... | collective-permute-start | bytes 522248 | tf_op jit(solution)/shard_map/ppermute | solution.py:175
  64.0 13.3 %all-to-all-start.1 = ((f16[8,2,32,512]{3,2,1,0:T(8,128)(2,1)}), f16[8,2,32,512]{3,2,1,0:T(8,128)(2,1)}, u32[]{:S(2)}, u32[]{:S(2)}) async-start(f16[8,2,32,512]{3,2,1,0:T(8,128)(2,1)} %convert_element_type.30), calls=%async_computation.1 | async-start | bytes 1048576 | tf_op jit(solution)/shard_map/all_to_all | solution.py:725
